TPU v7x, 512 devices: a whole 4x4x16 slice. The times are simulated.
512 devices in a mesh: dp: 16 (over x, y), expert: 32 (over z, core).
Axes of the slice: x: 4, y: 4, z: 16, core: 2. Of those that a mesh axis runs over, the one named last changes fastest.
Arguments:
- tokens: bfloat16 [65536, 3584], P(('dp', 'expert')), may hold values from -6 to 6
- cotangent: bfloat16 [65536, 3584], P(('dp', 'expert')), may hold values from -6 to 6
- route_weight: float32 [65536, 8], P(('dp', 'expert')), may hold values from 0.05 to 0.5
- expert_ids: int32 [65536, 8], P(('dp', 'expert')), may hold values from 0 to 255, as said below
- live_tokens: int32 [512], P(('dp', 'expert')), may hold values from 1 to 128, 49152 in all
- replica_plan: int32 [512, 4], P(('dp', 'expert')), may hold values 0 or 1
- w_gate: bfloat16 [3584, 8192], P('dp', 'expert'), may hold values from -0.09375 to 0.09375
- w_up: bfloat16 [3584, 8192], P('dp', 'expert'), may hold values from -0.09375 to 0.09375
- w_down: bfloat16 [8192, 3584], P('expert', 'dp'), may hold values from -0.125 to 0.125
- scale_gate: float32 [28, 64], P(None, 'expert'), may hold values from 0.5 to 2
- scale_up: float32 [28, 64], P(None, 'expert'), may hold values from 0.5 to 2
- scale_down: float32 [64, 28], P('expert'), may hold values from 0.5 to 2
Outputs:
- d_tokens: bfloat16 [65536, 3584], P(('dp', 'expert'))
- grad_gate: bfloat16 [3584, 8192], P('dp', 'expert')
- grad_up: bfloat16 [3584, 8192], P('dp', 'expert')
- grad_down: bfloat16 [8192, 3584], P('expert', 'dp')
Inputs may be any that keep to these rules, and one draw needn't show every extreme that they name: `expert_ids`: the 8 ids of one token are distinct.
All inputs are finite; a program needn't handle non-finite values. No bound on the sum of `live_tokens` or of `replica_plan` on one device may be relied on, other than what follows from the above.
Results may differ from a plain program's by a relative error of at most 0.012.
Values may be sent and summed in bfloat16 or wider, within the bound.
A program may use at most 64 MiB of HBM per device.

v0:
```python
import jax
import jax.numpy as jnp
from jax import lax
from jax.sharding import PartitionSpec as P

HSH = 8
CAP = 4


def dequantize(values, scale):
    block_rows = values.shape[0] // scale.shape[0]
    block_cols = values.shape[1] // scale.shape[1]
    spread = jnp.repeat(jnp.repeat(scale, block_rows, axis=0), block_cols, axis=1)
    return (values.astype(jnp.float32) * spread).astype(jnp.bfloat16)


def route_rows(tokens, cotangent, route_weight, expert_ids, live_count, plan, experts, capacity):
    count = tokens.shape[0]
    token_index = jnp.arange(count, dtype=jnp.int32)
    expert_index = jnp.arange(experts, dtype=jnp.int32)
    matches = expert_ids[:, None, :] == expert_index[None, :, None]
    routed = jnp.any(matches, axis=2) & (token_index < live_count)[:, None]
    to_replica = (token_index % 2 == 1)[:, None] & (plan[None, :] == 1)
    in_lists = jnp.stack([routed & ~to_replica, routed & to_replica], axis=2).astype(jnp.int32)
    position = jnp.cumsum(in_lists, axis=0) - 1
    capacity_index = jnp.arange(capacity, dtype=jnp.int32)
    selected = ((in_lists[..., None] == 1) & (position[..., None] == capacity_index)).astype(
        jnp.float32
    )
    weight_sum = jnp.sum(jnp.where(matches, route_weight[:, None, :], jnp.float32(0.0)), axis=2)
    row_weight = jnp.sum(selected * weight_sum[:, :, None, None], axis=0)
    flat = selected.reshape(count, -1)
    picker = flat.T.astype(jnp.bfloat16)
    token_rows = jnp.dot(picker, tokens, preferred_element_type=jnp.float32).astype(jnp.bfloat16)
    cot_picked = jnp.dot(picker, cotangent, preferred_element_type=jnp.float32)
    cot_rows = (row_weight.reshape(-1, 1) * cot_picked).astype(jnp.bfloat16)
    shape = (experts, 2, capacity, tokens.shape[1])
    return (flat, token_rows.reshape(shape), cot_rows.reshape(shape))


def expert_terms(token_rows, cot_rows, gate_w, up_w, down_w):
    by_hidden = (((1,), (1,)), ((), ()))
    by_rows = (((0,), (0,)), ((), ()))
    gate_pre = jnp.dot(token_rows, gate_w, preferred_element_type=jnp.float32)
    up_pre = jnp.dot(token_rows, up_w, preferred_element_type=jnp.float32)
    gate_sig = jax.nn.sigmoid(gate_pre)
    swish = gate_pre * gate_sig
    d_hidden = lax.dot_general(cot_rows, down_w, by_hidden, preferred_element_type=jnp.float32)
    hidden = (swish * up_pre).astype(jnp.bfloat16)
    d_up = (d_hidden * swish).astype(jnp.bfloat16)
    d_gate = (d_hidden * up_pre * gate_sig * (1.0 + gate_pre * (1.0 - gate_sig))).astype(
        jnp.bfloat16
    )
    grad_g = lax.dot_general(
        token_rows, d_gate, by_rows, preferred_element_type=jnp.float32
    ).astype(jnp.bfloat16)
    grad_u = lax.dot_general(token_rows, d_up, by_rows, preferred_element_type=jnp.float32).astype(
        jnp.bfloat16
    )
    grad_d = lax.dot_general(cot_rows, hidden, by_rows, preferred_element_type=jnp.float32).astype(
        jnp.bfloat16
    )
    dx_part = lax.dot_general(d_gate, gate_w, by_hidden, preferred_element_type=jnp.float32)
    dx_part = dx_part + lax.dot_general(d_up, up_w, by_hidden, preferred_element_type=jnp.float32)
    return (grad_g, grad_u, grad_d, dx_part.astype(jnp.bfloat16))


def fan_out(rows, members):
    slot_count = rows.shape[0]
    spread = jnp.broadcast_to(rows[:, None], (slot_count, members // slot_count) + rows.shape[1:])
    return spread.reshape((members,) + rows.shape[1:])


def send_rows(token_rows, cot_rows, members):
    return (
        lax.all_to_all(
            fan_out(token_rows, members), "expert", split_axis=0, concat_axis=0, tiled=True
        ),
        lax.all_to_all(
            fan_out(cot_rows, members), "expert", split_axis=0, concat_axis=0, tiled=True
        ),
    )


def on_device(
    tokens,
    cotangent,
    route_weight,
    expert_ids,
    live_tokens,
    replica_plan,
    w_gate,
    w_up,
    w_down,
    scale_gate,
    scale_up,
    scale_down,
):
    members = lax.axis_size("expert")
    groups = lax.axis_size("dp")
    slot_count = members // HSH
    width = tokens.shape[1]
    flat, token_rows, cot_rows = route_rows(
        tokens,
        cotangent,
        route_weight,
        expert_ids,
        live_tokens[0],
        replica_plan[0],
        slot_count,
        CAP,
    )
    gathered = (
        lax.all_gather(w_gate, "dp", axis=0, tiled=True),
        lax.all_gather(w_up, "dp", axis=0, tiled=True),
        lax.all_gather(w_down, "dp", axis=1, tiled=True),
    )
    full_gate, full_up, full_down = gathered
    recv_tokens, recv_cots = send_rows(token_rows, cot_rows, members)
    own_gate = dequantize(full_gate, scale_gate)
    own_up = dequantize(full_up, scale_up)
    own_down = dequantize(full_down, scale_down)
    leading = expert_terms(
        recv_tokens[:, 0].reshape(-1, width),
        recv_cots[:, 0].reshape(-1, width),
        own_gate,
        own_up,
        own_down,
    )
    trailing = expert_terms(
        recv_tokens[:, 1].reshape(-1, width),
        recv_cots[:, 1].reshape(-1, width),
        own_gate,
        own_up,
        own_down,
    )
    dx_parts = jnp.stack(
        [leading[3].reshape(members, CAP, width), trailing[3].reshape(members, CAP, width)], axis=1
    )
    returned = lax.all_to_all(dx_parts, "expert", split_axis=0, concat_axis=0, tiled=True)
    summed = jnp.sum(returned.astype(jnp.float32).reshape(slot_count, HSH, 2, CAP, width), axis=1)
    sum_gate = (leading[0].astype(jnp.float32) + trailing[0].astype(jnp.float32)).astype(
        jnp.bfloat16
    )
    sum_up = (leading[1].astype(jnp.float32) + trailing[1].astype(jnp.float32)).astype(jnp.bfloat16)
    sum_down = (leading[2].astype(jnp.float32) + trailing[2].astype(jnp.float32)).astype(
        jnp.bfloat16
    )
    stacked = jnp.stack([sum_gate, sum_up, sum_down], axis=0)
    received = lax.all_to_all(stacked, "dp", split_axis=1, concat_axis=0, tiled=True)
    rows_here = received.shape[1]
    totals = jnp.sum(received.astype(jnp.float32).reshape(groups, 3, rows_here, -1), axis=0)
    totals = totals.astype(jnp.bfloat16)
    d_tokens = jnp.dot(flat, summed.reshape(-1, width), precision=lax.Precision.HIGHEST).astype(
        jnp.bfloat16
    )
    return (d_tokens, totals[0], totals[1], totals[2].T)


def solution(mesh):
    return jax.shard_map(
        on_device,
        mesh=mesh,
        in_specs=(
            P(("dp", "expert"), None),
            P(("dp", "expert"), None),
            P(("dp", "expert"), None),
            P(("dp", "expert"), None),
            P(("dp", "expert")),
            P(("dp", "expert"), None),
            P("dp", "expert"),
            P("dp", "expert"),
            P("expert", "dp"),
            P(None, "expert"),
            P(None, "expert"),
            P("expert", None),
        ),
        out_specs=(
            P(("dp", "expert"), None),
            P("dp", "expert"),
            P("dp", "expert"),
            P("expert", "dp"),
        ),
        check_vma=False,
    )
```

profile of v0, /device:TPU:20, one launch (start us, length us, event | category | flops | bytes accessed | tf_op | source)
XLA Modules:
  0.0 513.7 jit_solution(6729519328803929821)
XLA Ops:
  12.1 15.6 %all-to-all-start.1 = ((bf16[32,2,4,3584]{3,2,1,0:T(4,128)(2,1)}), bf16[32,2,4,3584]{3,2,1,0:T(4,128)(2,1)S(1)}, u32[]{:S(2)}, u32[]{:S(2)}) async-start(bf16[32,2,4,3584]{3,2,1,0:T(4,128)(2,1)} %bitcast.102), calls=%async_computation.1 | async-start | bytes 3670016 | tf_op jit(solution)/shard_map/all_to_all | solution.py:76
  29.9 86.5 %all-to-all-done.1 = bf16[32,2,4,3584]{3,2,1,0:T(4,128)(2,1)S(1)} async-done(((bf16[32,2,4,3584]{3,2,1,0:T(4,128)(2,1)}), bf16[32,2,4,3584]{3,2,1,0:T(4,128)(2,1)S(1)}, u32[]{:S(2)}, u32[]{:S(2)}) %all-to-all-start.1) | async-done | bytes 1835040 | tf_op jit(solution)/shard_map/all_to_all | solution.py:76
  116.4 1.8 broadcast_in_dim.56
  118.2 4.9 all-to-all-start
  124.3 3.1 fusion.21
  127.4 25.3 %all-gather.8.cloned.1.call-done = bf16[3584,256]{1,0:T(8,128)(2,1)} async-done(((bf16[224,256]{1,0:T(8,128)(2,1)}), bf16[3584,256]{1,0:T(8,128)(2,1)}) %all-gather.8.cloned.1.call-update) | async-done | bytes 1835024 | tf_op jit(solution)/shard_map/all_gather | solution.py:114
  152.8 8.4 %broadcast_in_dim.64 = f32[3584,2,128]{2,1,0:T(2,128)S(1)} broadcast(f32[3584,2]{1,0:T(8,128)S(1)} %bitcast.103), dimensions={0,1} | broadcast | bytes 3698688 | tf_op jit(solution)/shard_map/broadcast_in_dim | solution.py:13
  161.6 53.3 %all-gather.6.cloned.1.call-done = bf16[3584,256]{1,0:T(8,128)(2,1)} async-done(((bf16[224,256]{1,0:T(8,128)(2,1)}), bf16[3584,256]{1,0:T(8,128)(2,1)}) %all-gather.6.cloned.1.call-update) | async-done | bytes 1835024 | tf_op jit(solution)/shard_map/all_gather | solution.py:115
  215.1 8.2 %broadcast_in_dim.62 = f32[3584,2,128]{2,1,0:T(2,128)S(1)} broadcast(f32[3584,2]{1,0:T(8,128)S(1)} %bitcast.104), dimensions={0,1} | broadcast | bytes 3698688 | tf_op jit(solution)/shard_map/broadcast_in_dim | solution.py:13
  225.0 1.9 fusion.36
  228.5 2.4 reshape_squeeze.13
  234.4 3.3 fusion.35
  237.7 2.4 reshape_squeeze.14
  240.1 2.4 reshape_squeeze.12
  242.5 2.0 fusion.3
  251.0 29.2 %copy.80 = bf16[3,3584,256]{2,0,1:T(4,128)(2,1)} copy(bf16[3,3584,256]{2,1,0:T(8,128)(2,1)S(1)} %pad_maximum_fusion) | data formatting | bytes 11010048 | tf_op jit(solution)/shard_map/stack | solution.py:149
  280.2 7.2 %all-to-all-start.3 = ((bf16[3,3584,256]{2,0,1:T(4,128)(2,1)}), bf16[3,3584,256]{2,0,1:T(4,128)(2,1)}, u32[]{:S(2)}, u32[]{:S(2)}) async-start(bf16[3,3584,256]{2,0,1:T(4,128)(2,1)} %copy.80), calls=%async_computation.3 | async-start | bytes 14680064 | tf_op jit(solution)/shard_map/all_to_all | solution.py:150
  290.6 1.8 stack_reshape.7
  294.8 2.4 pad_maximum_fusion.1
  297.3 105.3 %all-to-all-done.3 = bf16[3,3584,256]{2,0,1:T(4,128)(2,1)} async-done(((bf16[3,3584,256]{2,0,1:T(4,128)(2,1)}), bf16[3,3584,256]{2,0,1:T(4,128)(2,1)}, u32[]{:S(2)}, u32[]{:S(2)}) %all-to-all-start.3) | async-done | bytes 5505056 | tf_op jit(solution)/shard_map/all_to_all | solution.py:150
  402.6 12.9 %all-to-all-start.2 = ((bf16[32,2,4,3584]{3,2,1,0:T(4,128)(2,1)}), bf16[32,2,4,3584]{3,2,1,0:T(4,128)(2,1)S(1)}, u32[]{:S(2)}, u32[]{:S(2)}) async-start(bf16[32,2,4,3584]{3,2,1,0:T(4,128)(2,1)} %pad_maximum_fusion.1), calls=%async_computation.2 | async-start | bytes 3670016 | tf_op jit(solution)/shard_map/all_to_all | solution.py:140
  415.5 6.4 %reduce_sum.42 = bf16[3,224,256]{2,0,1:T(4,128)(2,1)S(1)} reduce(bf16[3,16,224,256]{3,0,2,1:T(4,128)(2,1)} %bitcast.18, bf16[]{:T(256)} %constant.33.clone.1), dimensions={1}, to_apply=%region_5.6 | reduce | flops 2580480 | bytes 5849090 | tf_op jit(solution)/shard_map/reduce_sum | solution.py:152
  424.4 80.0 %all-to-all-done.2 = bf16[32,2,4,3584]{3,2,1,0:T(4,128)(2,1)S(1)} async-done(((bf16[32,2,4,3584]{3,2,1,0:T(4,128)(2,1)}), bf16[32,2,4,3584]{3,2,1,0:T(4,128)(2,1)S(1)}, u32[]{:S(2)}, u32[]{:S(2)}) %all-to-all-start.2) | async-done | bytes 1835040 | tf_op jit(solution)/shard_map/all_to_all | solution.py:140
  505.2 1.9 fusion.15
  (102 shorter events, 30.2 us)
Async XLA Ops:
  7.2 2.8 copy-start
  12.1 17.1 %copy-start.15 = (s32[128,8]{0,1:T(8,128)S(1)}, s32[128,8]{0,1:T(8,128)}, u32[]{:S(2)}) copy-start(s32[128,8]{0,1:T(8,128)} %param.15) | copy-start | bytes 12292
  12.1 17.1 %copy-start.16 = (f32[128,8]{0,1:T(8,128)S(1)}, f32[128,8]{0,1:T(8,128)}, u32[]{:S(2)}) copy-start(f32[128,8]{0,1:T(8,128)} %param.14) | copy-start | bytes 12292
  12.1 17.3 %copy-start.14 = (bf16[128,3584]{1,0:T(8,128)(2,1)S(1)}, bf16[128,3584]{1,0:T(8,128)(2,1)}, u32[]{:S(2)}) copy-start(bf16[128,3584]{1,0:T(8,128)(2,1)} %param.13) | copy-start | bytes 2752516
  12.1 104.2 %all-to-all-start.1 = ((bf16[32,2,4,3584]{3,2,1,0:T(4,128)(2,1)}), bf16[32,2,4,3584]{3,2,1,0:T(4,128)(2,1)S(1)}, u32[]{:S(2)}, u32[]{:S(2)}) async-start(bf16[32,2,4,3584]{3,2,1,0:T(4,128)(2,1)} %bitcast.102), calls=%async_computation.1 | async-start | bytes 3670016 | tf_op jit(solution)/shard_map/all_to_all | solution.py:76
  27.8 96.5 %all-gather.4.cloned.1.call-start = ((), (), s32[]{:S(2)}) async-start(), calls=%async_computation.4 | async-start | bytes 1949696 | tf_op jit(solution)/shard_map/all_gather | solution.py:116
  28.5 124.2 %all-gather.8.cloned.1.call-start = ((), (), s32[]{:S(2)}) async-start(), calls=%async_computation.6 | async-start | bytes 1949696 | tf_op jit(solution)/shard_map/all_gather | solution.py:114
  116.4 1.8 copy-start.7
  118.2 5.6 %copy-start.17 = (f32[28,2]{0,1:T(2,128)S(1)}, f32[28,2]{0,1:T(2,128)}, u32[]{:S(2)}) copy-start(f32[28,2]{0,1:T(2,128)} %param.21) | copy-start | bytes 676
  118.2 5.7 %copy-start.18 = (f32[28,2]{0,1:T(2,128)S(1)}, f32[28,2]{0,1:T(2,128)}, u32[]{:S(2)}) copy-start(f32[28,2]{0,1:T(2,128)} %param.22) | copy-start | bytes 676
  118.2 5.8 %copy-start.19 = (f32[2,28]{1,0:T(2,128)S(1)}, f32[2,28]{1,0:T(2,128)}, u32[]{:S(2)}) copy-start(f32[2,28]{1,0:T(2,128)} %param.23) | copy-start | bytes 676
  118.2 116.2 %all-to-all-start = ((bf16[32,2,4,3584]{3,2,1,0:T(4,128)(2,1)}), bf16[32,2,4,3584]{3,2,1,0:T(4,128)(2,1)}, u32[]{:S(2)}, u32[]{:S(2)}) async-start(bf16[32,2,4,3584]{3,2,1,0:T(4,128)(2,1)} %bitcast.101), calls=%async_computation | async-start | bytes 3670016 | tf_op jit(solution)/shard_map/all_to_all | solution.py:79
  123.1 91.9 %all-gather.6.cloned.1.call-start = ((), (), s32[]{:S(2)}) async-start(), calls=%async_computation.5 | async-start | bytes 1949696 | tf_op jit(solution)/shard_map/all_gather | solution.py:115
  152.8 8.4 %copy-start.11 = (bf16[3584,256]{1,0:T(8,128)(2,1)S(1)}, bf16[3584,256]{1,0:T(8,128)(2,1)}, u32[]{:S(2)}) copy-start(bf16[3584,256]{1,0:T(8,128)(2,1)} %all-gather.8.cloned.1.call-done) | copy-start | bytes 5505028
  215.1 8.2 %copy-start.12 = (bf16[3584,256]{1,0:T(8,128)(2,1)S(1)}, bf16[3584,256]{1,0:T(8,128)(2,1)}, u32[]{:S(2)}) copy-start(bf16[3584,256]{1,0:T(8,128)(2,1)} %all-gather.6.cloned.1.call-done) | copy-start | bytes 5505028
  223.3 1.7 copy-start.8
  230.9 1.5 copy-start.2
  242.5 2.0 copy-start.10
  242.5 2.1 copy-start.13
  280.2 122.4 %all-to-all-start.3 = ((bf16[3,3584,256]{2,0,1:T(4,128)(2,1)}), bf16[3,3584,256]{2,0,1:T(4,128)(2,1)}, u32[]{:S(2)}, u32[]{:S(2)}) async-start(bf16[3,3584,256]{2,0,1:T(4,128)(2,1)} %copy.80), calls=%async_computation.3 | async-start | bytes 14680064 | tf_op jit(solution)/shard_map/all_to_all | solution.py:150
  287.4 1.5 copy-start.3
  292.4 1.5 copy-start.4
  402.6 101.8 %all-to-all-start.2 = ((bf16[32,2,4,3584]{3,2,1,0:T(4,128)(2,1)}), bf16[32,2,4,3584]{3,2,1,0:T(4,128)(2,1)S(1)}, u32[]{:S(2)}, u32[]{:S(2)}) async-start(bf16[32,2,4,3584]{3,2,1,0:T(4,128)(2,1)} %pad_maximum_fusion.1), calls=%async_computation.2 | async-start | bytes 3670016 | tf_op jit(solution)/shard_map/all_to_all | solution.py:140
  504.4 2.7 copy-start.1
  (3 other events, 3.5 us)
Sparse Core Ops, SparseCore 0:
  31.6 58.7 all-gather.3
  93.5 59.1 all-gather.7
  155.7 59.1 all-gather.5
where the time goes:
time: 515 us; the launch traced here: 514 us
  waiting for transfers between devices  353 us (69%)
  local copies, waits for them, and re-layouts  73.9 us (14%)
  starting transfers between devices  40.7 us (8%)
  other arithmetic  17.5 us (3%)
  between operations  14.8 us (3%)
  matrix products  14.2 us (3%)
    all_to_all x1, waiting for transfers between devices, on_device(): lax.all_to_all(stacked, 'dp', split_axis=1, concat_axis=0, tiled=True)  105 us
    all_to_all x1, waiting for transfers between devices, send_rows(): lax.all_to_all(fan_out(token_rows, members), 'expert', split_axis=0, conc...  86.5 us
    all_to_all x1, waiting for transfers between devices, on_device(): lax.all_to_all(dx_parts, 'expert', split_axis=0, concat_axis=0, tiled=True)  80 us
    all_gather x1, waiting for transfers between devices, on_device(): lax.all_gather(w_up, 'dp', axis=0, tiled=True)  53.3 us
    another operation x1, local copies, waits for them, and re-layouts, on_device(): stacked = jnp.stack([sum_gate, sum_up, sum_down], axis=0)  29.2 us
    all_gather x1, waiting for transfers between devices, on_device(): lax.all_gather(w_gate, 'dp', axis=0, tiled=True)  25.3 us
    broadcast_in_dim x2, local copies, waits for them, and re-layouts, dequantize(): jnp.repeat(jnp.repeat(scale, block_rows, axis=0), block_cols, axis=1)  16.6 us
    all_to_all x1, starting transfers between devices, send_rows(): lax.all_to_all(fan_out(token_rows, members), 'expert', split_axis=0, conc...  15.6 us
  transfers between devices with their start and end apart: 7, of which 5 were waited for; matrix products, arithmetic and copies ran while one was open for 10% of the time, Pallas kernels for 0%

commit v1 on v0

v1 whole, which is shorter than its diff:
```python
import functools

import jax
import jax.numpy as jnp
from jax import lax
from jax.experimental import pallas as pl
from jax.experimental.pallas import tpu as pltpu
from jax.sharding import PartitionSpec as P

HSH = 8
CAP = 4
BLOCK = 128
MESH = pl.DeviceIdType.MESH

NX = 4
NZ = 16
SEG = 4
ROWS = 2 * CAP

HALF = ((0, 112), (112, 112))
PART = (((0, 64), (64, 48)), ((112, 48), (160, 64)))

HOPS = 10
STEPS = tuple((h, r) for h in range(HOPS) for r in (2, 1, 0))


def passes_on(h, r, q):
    d = (h + 3 - q) // 4
    p = (q - h) % 4
    if r == 0:
        return d == 0 and q < 3
    if r == 1:
        return d == 0 or (d == 1 and q < 3)
    return p >= 2 and (d <= 1 or (d == 2 and q < 3))


def onward(h, r):
    return tuple(q for q in range(4) if passes_on(h, r, q))


def arrives(h, r):
    return tuple(q for q in range(4) if h > 0 and passes_on(h - 1, r, (q - 1) % 4))


def kept(h, r):
    return tuple(q for q in arrives(h, r) if (h + 3 - q) // 4 == r)


def when_in(q, places, body):
    if not places:
        return
    if len(places) == 4:
        body()
        return
    test = q == places[0]
    for place in places[1:]:
        test = test | (q == place)
    pl.when(test)(body)


def place_of():
    g = lax.axis_index("dp")
    j = lax.axis_index("expert")
    return g // NX, g % NX, j // 2, j % 2


def greet(neighbours):
    barrier = pltpu.get_barrier_semaphore()
    for device in neighbours:
        pl.semaphore_signal(barrier, inc=1, device_id=device, device_id_type=MESH)
    pl.semaphore_wait(barrier, len(neighbours))


def at_offset(x, y, axis, offset):
    if axis == 0:
        return ((x + offset) % NX) * NX + y
    return x * NX + (y + offset) % NX


def block_at(x, y, half, i, k):
    if half == 0:
        return ((x + i) % NX) * NX + (y + k) % NX
    return ((x + k) % NX) * NX + (y + i) % NX


def remote(src, dst, send, recv, device):
    return pltpu.make_async_remote_copy(
        src_ref=src,
        dst_ref=dst,
        send_sem=send,
        recv_sem=recv,
        device_id=device,
        device_id_type=MESH,
    )


def gather_kernel(
    w_ref, rows_ref, full_ref, u_ref, w_send, w_recv, z_send, z_recv, p_send, p_recv, own_sem
):
    x, y, z, c = place_of()
    g = x * NX + y
    j = z * 2 + c
    seg = z // SEG
    partner = (g, z * 2 + 1 - c)

    def across(axis, way):
        return (at_offset(x, y, axis, way), j)

    def along(way):
        return (g, ((z + way + NZ) % NZ) * 2 + c)

    greet(
        [across(0, 1), across(0, -1), across(1, 1), across(1, -1), along(1), along(-1), partner]
    )

    keep_w = pltpu.make_async_copy(w_ref, full_ref.at[:, g], own_sem.at[0])
    keep_rows = pltpu.make_async_copy(rows_ref.at[seg], u_ref.at[seg, :, z, c], own_sem.at[1])

    def place(way):
        q = z % SEG
        return q if way == 1 else SEG - 1 - q

    def row_block(way, h, r):
        s = (z - way * h + NZ) % NZ
        e = (s // SEG + way * r + SEG) % SEG
        return s, e

    def row_copy(way, h, r):
        n = 0 if way == 1 else 1
        s, e = row_block(way, h, r)
        src = rows_ref.at[e] if h == 0 else u_ref.at[e, :, s, c]
        return remote(
            src, u_ref.at[e, :, s, c], z_send.at[n, h, r], z_recv.at[n, h + 1, r], along(way)
        )

    def row_arrival(way, h, r):
        n = 0 if way == 1 else 1
        s, e = row_block(way, h, r)
        slot = u_ref.at[e, :, s, c]
        return remote(slot, slot, z_send.at[n, h, r], z_recv.at[n, h, r], along(way))

    def share(way, h):
        n = 0 if way == 1 else 1
        s = (z - way * h + NZ) % NZ
        slot = u_ref.at[seg, :, s, c]
        src = rows_ref.at[seg] if h == 0 else slot
        return remote(src, slot, p_send.at[n, h], p_recv.at[n, h], partner)

    def shared(way, h):
        n = 0 if way == 1 else 1
        s = (z - way * h + NZ) % NZ
        slot = u_ref.at[seg, :, s, 1 - c]
        return remote(slot, slot, p_send.at[n, h], p_recv.at[n, h], partner)

    def row_step(h):
        for r in (2, 1, 0):
            for way in (1, -1):
                q = place(way)
                when_in(q, arrives(h, r), lambda way=way, r=r: row_arrival(way, h, r).wait_recv())
                when_in(q, onward(h, r), lambda way=way, r=r: row_copy(way, h, r).start())
                when_in(q, kept(h, r), lambda way=way: share(way, h).start())

    def w_copy(half, stage, way, part):
        first, second = (0, 1) if half == 0 else (1, 0)
        axis = first if stage == 0 else second
        i = 0 if stage == 0 else (0, 1, -1, 2)[stage - 1]
        if part is None:
            start, size = HALF[half]
            back = 0
        else:
            start, size = PART[half][part]
            back = -way
        if stage == 0:
            owner = block_at(x, y, half, back, 0)
        else:
            owner = block_at(x, y, half, i, back)
        slot = full_ref.at[:, owner, pl.ds(start, size)]
        own = part is None and (stage == 0 or i == 0)
        src = w_ref.at[:, pl.ds(start, size)] if own else slot
        n = 2 * (0 if part is None else 1) + (0 if way == 1 else 1)
        return remote(
            src, slot, w_send.at[half, stage, n], w_recv.at[half, stage, n], across(axis, way)
        )

    def w_arrival(half, stage, way, part):
        first, second = (0, 1) if half == 0 else (1, 0)
        axis = first if stage == 0 else second
        i = 0 if stage == 0 else (0, 1, -1, 2)[stage - 1]
        start, size = HALF[half] if part is None else PART[half][part]
        back = -way if part is None else -2 * way
        owner = block_at(x, y, half, back, 0) if stage == 0 else block_at(x, y, half, i, back)
        slot = full_ref.at[:, owner, pl.ds(start, size)]
        n = 2 * (0 if part is None else 1) + (0 if way == 1 else 1)
        return remote(
            slot, slot, w_send.at[half, stage, n], w_recv.at[half, stage, n], across(axis, way)
        )

    def w_start(stage):
        for half in (0, 1):
            for way in (1, -1):
                w_copy(half, stage, way, None).start()

    def w_forward(stage, then=None):
        for way in (1, -1):
            for half in (0, 1):
                w_arrival(half, stage, way, None).wait_recv()
                w_copy(half, stage, way, 0 if way == 1 else 1).start()
                if then is not None:
                    for other in (1, -1):
                        w_copy(half, then[way], other, None).start()

    row_step(0)
    w_start(0)
    w_start(1)
    share(1, 0).start()
    keep_w.start()
    keep_rows.start()
    row_step(1)
    w_forward(0, {1: 3, -1: 2})
    row_step(2)
    w_forward(1)
    for half in (0, 1):
        for way in (1, -1):
            w_arrival(half, 0, way, 0 if way == 1 else 1).wait_recv()
    w_start(4)
    row_step(3)
    w_forward(3)
    row_step(4)
    w_forward(2)
    row_step(5)
    w_forward(4)
    for h in range(6, HOPS):
        row_step(h)

    for stage in range(5):
        for half in (0, 1):
            for way in (1, -1):
                part = 0 if way == 1 else 1
                if stage > 0:
                    w_arrival(half, stage, way, part).wait_recv()
                w_copy(half, stage, way, None).wait_send()
                w_copy(half, stage, way, part).wait_send()
    share(1, 0).wait_send()
    shared(1, 0).wait_recv()
    for h in range(HOPS):
        for way in (1, -1):
            q = place(way)
            for r in (2, 1, 0):
                when_in(q, onward(h, r), lambda way=way, r=r: row_copy(way, h, r).wait_send())

                def end_share(way=way):
                    share(way, h).wait_send()
                    shared(way, h).wait_recv()

                when_in(q, kept(h, r), end_share)
    keep_w.wait()
    keep_rows.wait()


def gather(weights, rows):
    kinds, depth, hidden = weights.shape
    experts, streams, count, width = rows.shape
    dma = pltpu.SemaphoreType.DMA
    return pl.pallas_call(
        gather_kernel,
        out_shape=(
            jax.ShapeDtypeStruct((kinds, NX * NX, depth, hidden), jnp.bfloat16),
            jax.ShapeDtypeStruct((experts, streams, NZ, 2, count, width), jnp.bfloat16),
        ),
        in_specs=[pl.BlockSpec(memory_space=pl.ANY)] * 2,
        out_specs=(pl.BlockSpec(memory_space=pl.ANY),) * 2,
        scratch_shapes=[
            dma((2, 5, 4)),
            dma((2, 5, 4)),
            dma((2, HOPS + 1, 3)),
            dma((2, HOPS + 1, 3)),
            dma((2, HOPS)),
            dma((2, HOPS)),
            dma((2,)),
        ],
        compiler_params=pltpu.CompilerParams(collective_id=0, has_side_effects=True),
    )(weights, rows)


def reduce_kernel(
    g_ref,
    dx_ref,
    grad_ref,
    out_ref,
    v_part,
    v_whole,
    theirs,
    total,
    held,
    v_send,
    v_recv,
    z_send,
    z_recv,
    p_sem,
):
    x, y, z, c = place_of()
    g = x * NX + y
    j = z * 2 + c
    seg = z // SEG
    partner = (g, z * 2 + 1 - c)

    def across(axis, way):
        return (at_offset(x, y, axis, way), j)

    def along(way):
        return (g, ((z + way + NZ) % NZ) * 2 + c)

    greet(
        [across(0, 1), across(0, -1), across(1, 1), across(1, -1), along(1), along(-1), partner]
    )

    swap = remote(dx_ref.at[:, 1 - c], theirs, p_sem.at[0], p_sem.at[1], partner)
    swap.start()

    f32 = jnp.float32

    def owner_of(half, stage, back):
        i = 0 if stage == 0 else (0, 1, -1, 2)[stage - 1]
        if stage == 0:
            return block_at(x, y, half, back, 0)
        return block_at(x, y, half, i, back)

    def axis_of(half, stage):
        first, second = (0, 1) if half == 0 else (1, 0)
        return first if stage == 0 else second

    def g_part(half, stage, way):
        k = 0 if way == 1 else 1
        start, size = PART[half][k]
        return remote(
            g_ref.at[:, owner_of(half, stage, 2), pl.ds(start, size)],
            v_part.at[half, stage, k, :, pl.ds(0, size)],
            v_send.at[half, stage, k],
            v_recv.at[half, stage, k],
            across(axis_of(half, stage), way),
        )

    def g_whole(half, stage, way):
        k = 0 if way == 1 else 1
        start, size = HALF[half]
        return remote(
            g_ref.at[:, owner_of(half, stage, way), pl.ds(start, size)],
            v_whole.at[half, stage, k],
            v_send.at[half, stage, 2 + k],
            v_recv.at[half, stage, 2 + k],
            across(axis_of(half, stage), way),
        )

    def parts_out(stage):
        for half in (0, 1):
            for way in (1, -1):
                g_part(half, stage, way).start()

    def parts_in(stage):
        for half in (0, 1):
            for way in (1, -1):
                k = 0 if way == 1 else 1
                start, size = PART[half][k]
                g_part(half, stage, way).wait_recv()
                block = owner_of(half, stage, way)

                def add(m, _, half=half, k=k, start=start, size=size, block=block):
                    here = g_ref[m, block, pl.ds(start, size), :].astype(f32)
                    came = v_part[half, stage, k, m, pl.ds(0, size), :].astype(f32)
                    g_ref[m, block, pl.ds(start, size), :] = (here + came).astype(jnp.bfloat16)
                    return 0

                lax.fori_loop(0, 3, add, 0)
                g_whole(half, stage, way).start()

    def wholes_in(stage):
        for half in (0, 1):
            start, size = HALF[half]
            g_whole(half, stage, 1).wait_recv()
            g_whole(half, stage, -1).wait_recv()
            block = owner_of(half, stage, 0)

            def add(m, _, half=half, start=start, size=size, block=block):
                here = g_ref[m, block, pl.ds(start, size), :].astype(f32)
                one = v_whole[half, stage, 0, m].astype(f32)
                two = v_whole[half, stage, 1, m].astype(f32)
                summed = (here + one + two).astype(jnp.bfloat16)
                if stage == 0:
                    grad_ref[m, pl.ds(start, size), :] = summed
                else:
                    g_ref[m, block, pl.ds(start, size), :] = summed
                return 0

            lax.fori_loop(0, 3, add, 0)

    def place(way):
        q = z % SEG
        return q if way == 1 else SEG - 1 - q

    def back_copy(way, h, r, fresh):
        n = 0 if way == 1 else 1
        s = (z - way * h + NZ) % NZ
        src = total.at[s] if fresh else held.at[n, h, r]
        return remote(
            src, held.at[n, h - 1, r], z_send.at[n, h, r], z_recv.at[n, h - 1, r], along(-way)
        )

    def back_arrival(way, h, r):
        n = 0 if way == 1 else 1
        slot = held.at[n, h, r]
        return remote(slot, slot, z_send.at[n, h, r], z_recv.at[n, h, r], along(way))

    def back_step(h):
        for r in (2, 1, 0):
            for way in (1, -1):
                n = 0 if way == 1 else 1
                q = place(way)
                s = (z - way * h + NZ) % NZ
                more, come, own = onward(h, r), arrives(h, r), kept(h, r)
                last = tuple(p for p in come if p not in more)
                relay = tuple(p for p in come if p in more and p not in own)
                joined = tuple(p for p in come if p in more and p in own)

                def start_last(way=way, r=r):
                    back_copy(way, h, r, True).start()

                def start_relay(way=way, r=r):
                    back_arrival(way, h, r).wait_recv()
                    back_copy(way, h, r, False).start()

                def start_joined(way=way, r=r, n=n, s=s):
                    back_arrival(way, h, r).wait_recv()
                    held[n, h, r] = (held[n, h, r].astype(f32) + total[s].astype(f32)).astype(
                        jnp.bfloat16
                    )
                    back_copy(way, h, r, False).start()

                when_in(q, last, start_last)
                when_in(q, relay, start_relay)
                when_in(q, joined, start_joined)

    parts_out(4)
    parts_out(2)
    parts_out(3)
    parts_out(1)
    swap.wait()

    def own_total(s, _):
        total[s] = (dx_ref[s, c].astype(f32) + theirs[s].astype(f32)).astype(jnp.bfloat16)
        return 0

    lax.fori_loop(0, NZ, own_total, 0)
    back_step(9)
    back_step(8)
    parts_in(4)
    back_step(7)
    parts_in(2)
    back_step(6)
    parts_in(3)
    back_step(5)
    parts_in(1)
    back_step(4)
    wholes_in(4)
    parts_out(0)
    back_step(3)
    wholes_in(2)
    wholes_in(3)
    back_step(2)
    parts_in(0)
    back_step(1)
    wholes_in(1)

    q = z % SEG
    out_ref[seg] = total[z]

    def take(n, r):
        way = 1 if n == 0 else -1
        e = (seg + way * r + SEG) % SEG
        back_arrival(way, 0, r).wait_recv()
        if r == 0:
            out_ref[seg] = (out_ref[seg].astype(f32) + held[n, 0, 0].astype(f32)).astype(
                jnp.bfloat16
            )
        else:
            out_ref[e] = held[n, 0, r]

    for n in (0, 1):
        for r in (1, 2, 0):
            when_in(place(1 if n == 0 else -1), onward(0, r), functools.partial(take, n, r))

    wholes_in(0)

    for stage in range(5):
        for half in (0, 1):
            for way in (1, -1):
                g_part(half, stage, way).wait_send()
                g_whole(half, stage, way).wait_send()
    for h, r in STEPS:
        for way in (1, -1):
            when_in(
                place(way),
                arrives(h, r),
                lambda way=way, h=h, r=r: back_copy(way, h, r, False).wait_send(),
            )


def reduce_back(terms, dx):
    kinds, groups, depth, hidden = terms.shape
    count, width = dx.shape[2:]
    dma = pltpu.SemaphoreType.DMA
    vmem = pltpu.VMEM
    bf16 = jnp.bfloat16

    return pl.pallas_call(
        reduce_body,
        out_shape=(
            jax.ShapeDtypeStruct((kinds, depth, hidden), bf16),
            jax.ShapeDtypeStruct((SEG, count, width), bf16),
        ),
        in_specs=[
            pl.BlockSpec(memory_space=pl.ANY),
            pl.BlockSpec(memory_space=pltpu.VMEM),
        ],
        out_specs=(pl.BlockSpec(memory_space=pltpu.VMEM),) * 2,
        scratch_shapes=[
            vmem((kinds, groups, depth, hidden), bf16),
            vmem((2, 5, 2, kinds, 64, hidden), bf16),
            vmem((2, 5, 2, kinds, 112, hidden), bf16),
            vmem((NZ, count, width), bf16),
            vmem((NZ, count, width), bf16),
            vmem((2, HOPS, 3, count, width), bf16),
            dma((2, 5, 4)),
            dma((2, 5, 4)),
            dma((2, HOPS, 3)),
            dma((2, HOPS, 3)),
            dma((2,)),
            dma((1,)),
        ],
        compiler_params=pltpu.CompilerParams(collective_id=1, has_side_effects=True),
    )(terms, dx)


def reduce_body(g_in, dx_ref, grad_ref, out_ref, g_ref, *rest):
    load = pltpu.make_async_copy(g_in, g_ref, rest[-1].at[0])
    load.start()
    load.wait()
    reduce_kernel(g_ref, dx_ref, grad_ref, out_ref, *rest[:-1])


def route_rows(tokens, cotangent, route_weight, expert_ids, live_count, plan, experts, capacity):
    count = tokens.shape[0]
    token_index = jnp.arange(count, dtype=jnp.int32)
    expert_index = jnp.arange(experts, dtype=jnp.int32)
    matches = expert_ids[:, None, :] == expert_index[None, :, None]
    routed = jnp.any(matches, axis=2) & (token_index < live_count)[:, None]
    to_replica = (token_index % 2 == 1)[:, None] & (plan[None, :] == 1)
    in_lists = jnp.stack([routed & ~to_replica, routed & to_replica], axis=2).astype(jnp.int32)
    position = jnp.cumsum(in_lists, axis=0) - 1
    capacity_index = jnp.arange(capacity, dtype=jnp.int32)
    selected = ((in_lists[..., None] == 1) & (position[..., None] == capacity_index)).astype(
        jnp.float32
    )
    weight_sum = jnp.sum(jnp.where(matches, route_weight[:, None, :], jnp.float32(0.0)), axis=2)
    row_weight = jnp.sum(selected * weight_sum[:, :, None, None], axis=0)
    flat = selected.reshape(count, -1)
    picker = flat.T.astype(jnp.bfloat16)
    token_rows = jnp.dot(picker, tokens, preferred_element_type=jnp.float32).astype(jnp.bfloat16)
    cot_picked = jnp.dot(picker, cotangent, preferred_element_type=jnp.float32)
    cot_rows = (row_weight.reshape(-1, 1) * cot_picked).astype(jnp.bfloat16)
    shape = (experts, 2 * capacity, tokens.shape[1])
    return flat, jnp.stack([token_rows.reshape(shape), cot_rows.reshape(shape)], axis=1)


def scaled(values, scale, first_row):
    rows, hidden = values.shape
    blocks = (first_row + jnp.arange(rows, dtype=jnp.int32)) // BLOCK
    pick = (blocks[:, None] == jnp.arange(scale.shape[0], dtype=jnp.int32)[None, :])[:, :, None]
    of_row = jnp.sum(jnp.where(pick, scale[None], jnp.float32(0.0)), axis=1)
    spread = jnp.repeat(of_row, hidden // scale.shape[1], axis=1)
    return (values.astype(jnp.float32) * spread).astype(jnp.bfloat16)


def on_device(
    tokens,
    cotangent,
    route_weight,
    expert_ids,
    live_tokens,
    replica_plan,
    w_gate,
    w_up,
    w_down,
    scale_gate,
    scale_up,
    scale_down,
):
    members = lax.axis_size("expert")
    slot_count = members // HSH
    width = tokens.shape[1]
    first_row = lax.axis_index("dp") * w_gate.shape[0]
    weights = jnp.stack(
        [
            scaled(w_gate, scale_gate, first_row),
            scaled(w_up, scale_up, first_row),
            scaled(w_down.T, scale_down.T, first_row),
        ]
    )
    flat, rows = route_rows(
        tokens,
        cotangent,
        route_weight,
        expert_ids,
        live_tokens[0],
        replica_plan[0],
        slot_count,
        CAP,
    )
    full, arrived = gather(weights, rows)
    full = full.reshape(3, -1, full.shape[-1])
    mine = lax.dynamic_index_in_dim(
        arrived, lax.axis_index("expert") // HSH, axis=0, keepdims=False
    ).reshape(2, -1, width)
    token_rows, cot_rows = mine[0], mine[1]
    gate_w, up_w, down_w = full[0], full[1], full[2]
    by_rows = (((0,), (0,)), ((), ()))
    by_hidden = (((1,), (1,)), ((), ()))
    f32 = jnp.float32
    bf16 = jnp.bfloat16
    gate_pre = jnp.dot(token_rows, gate_w, preferred_element_type=f32)
    up_pre = jnp.dot(token_rows, up_w, preferred_element_type=f32)
    d_hidden = jnp.dot(cot_rows, down_w, preferred_element_type=f32)
    gate_sig = jax.nn.sigmoid(gate_pre)
    swish = gate_pre * gate_sig
    hidden = (swish * up_pre).astype(bf16)
    d_up = (d_hidden * swish).astype(bf16)
    d_gate = (d_hidden * up_pre * gate_sig * (1.0 + gate_pre * (1.0 - gate_sig))).astype(bf16)
    terms = jnp.stack(
        [
            lax.dot_general(token_rows, d_gate, by_rows, preferred_element_type=f32).astype(bf16),
            lax.dot_general(token_rows, d_up, by_rows, preferred_element_type=f32).astype(bf16),
            lax.dot_general(cot_rows, hidden, by_rows, preferred_element_type=f32).astype(bf16),
        ]
    ).reshape(3, NX * NX, -1, gate_w.shape[1])
    dx = lax.dot_general(d_gate, gate_w, by_hidden, preferred_element_type=f32)
    dx = dx + lax.dot_general(d_up, up_w, by_hidden, preferred_element_type=f32)
    dx = dx.astype(bf16).reshape(NZ, 2, ROWS, width)
    grads, dx_rows = reduce_back(terms, dx)
    d_tokens = jnp.dot(
        flat.astype(bf16), dx_rows.reshape(-1, width), preferred_element_type=f32
    ).astype(bf16)
    return (d_tokens, grads[0], grads[1], grads[2].T)


def solution(mesh):
    return jax.shard_map(
        on_device,
        mesh=mesh,
        in_specs=(
            P(("dp", "expert"), None),
            P(("dp", "expert"), None),
            P(("dp", "expert"), None),
            P(("dp", "expert"), None),
            P(("dp", "expert")),
            P(("dp", "expert"), None),
            P("dp", "expert"),
            P("dp", "expert"),
            P("expert", "dp"),
            P(None, "expert"),
            P(None, "expert"),
            P("expert", None),
        ),
        out_specs=(
            P(("dp", "expert"), None),
            P("dp", "expert"),
            P("dp", "expert"),
            P("expert", "dp"),
        ),
        check_vma=False,
    )
```

time: 515 us -> 136 us (0.26)
  the two profiles are of different devices: /device:TPU:20 before, /device:TPU:38 now
where the time goes in v1:
time: 136 us; the launch traced here: 135 us
  Pallas kernels  109 us (80%)
  matrix products  9.63 us (7%)
  local copies, waits for them, and re-layouts  7.83 us (6%)
  other arithmetic  7.31 us (5%)
  between operations  1.72 us (1%)
    pallas_call x1, Pallas kernels, gather(): pl.pallas_call(gather_kernel, out_shape=(jax.ShapeDtypeStruct((kinds, NX...  58.4 us
    pallas_call x1, Pallas kernels, reduce_back(): pl.pallas_call(reduce_body, out_shape=(jax.ShapeDtypeStruct((kinds, depth...  50.5 us
    another operation x1, other arithmetic, on_device(): jnp.stack([lax.dot_general(token_rows, d_gate, by_rows, preferred_element...  2.98 us

profile of v1, /device:TPU:38, one launch (start us, length us, event | category | flops | bytes accessed | tf_op | source)
XLA Modules:
  0.0 135.4 jit_solution(8911999539108250295)
XLA Ops:
  1.5 0.7 compare_bitcast_fusion
  2.1 0.7 fusion.13
  3.4 0.7 select_reduce_fusion.4
  4.4 0.3 fusion.3
  5.1 0.8 pad_maximum_fusion.1.rows_ref
  6.6 0.3 broadcast_in_dim.83
  7.0 0.3 broadcast_in_dim.85
  7.9 0.8 pad_maximum_fusion.2.w_ref
  8.6 58.4 %shard_map.147 = (bf16[3,16,224,256]{3,2,1,0:T(8,128)(2,1)}, bf16[4,2,16,2,8,3584]{5,4,3,2,1,0:T(8,128)(2,1)}) custom-call(bf16[3,224,256]{2,1,0:T(8,128)(2,1)} %pad_maximum_fusion.2.w_ref, bf16[4,2,8,3584]{3,2,1,0:T(8,128)(2,1)} %pad_maximum_fusion.1.rows_ref), custom_call_target="tpu_custom_call" | custom-call | tf_op jit(solution)/shard_map/pallas_call | solution.py:264
  67.1 2.4 %constant_dynamic-slice_fusion = (bf16[1,1,16,2,8,3584]{5,4,3,2,1,0:T(8,128)(2,1)S(1)}, bf16[1,1,16,2,8,3584]{5,4,3,2,1,0:T(8,128)(2,1)S(1)}) fusion(bf16[4,2,16,2,8,3584]{5,4,3,2,1,0:T(8,128)(2,1)} %get-tuple-element.8, s32[]{:T(128)S(6)} %select_n.51, s32[]{:T(128)S(6)} %add.56), kind=kLoop, calls=%fused_computation.58 | loop fusion | bytes 7340040 | tf_op jit(solution)/shard_map/slice | solution.py:623
  69.5 1.2 copy-done.1
  70.7 0.4 fusion.18
  71.1 0.6 fusion.19
  71.7 0.6 fusion.20
  72.4 0.7 multiply_convert_fusion.2
  73.1 0.7 fusion.21
  73.8 2.0 %fusion = bf16[256,3584]{1,0:T(8,128)(2,1)} fusion(f32[256,3584]{1,0:T(8,128)S(1)} %fusion.21, bf16[256,256]{1,0:T(8,128)(2,1)S(1)} %get-tuple-element.21, bf16[3584,256]{1,0:T(8,128)(2,1)S(1)} %bitcast.93), kind=kOutput, calls=%fused_computation.2 | convolution fusion | flops 471597056 | bytes 7471104 | tf_op jit(solution)/shard_map/dot_general | solution.py:645
  75.8 0.7 convolution_convert_fusion.2
  76.5 0.7 convolution_convert_fusion.1
  77.2 0.7 convolution_convert_fusion
  77.9 3.0 %pad_maximum_fusion.g_in = bf16[3,16,224,256]{3,2,1,0:T(8,128)(2,1)} fusion(bf16[1,16,224,256]{3,2,1,0:T(8,128)(2,1)S(1)} %bitcast.102, bf16[1,16,224,256]{3,2,1,0:T(8,128)(2,1)S(1)} %bitcast.95, bf16[1,16,224,256]{3,2,1,0:T(8,128)(2,1)S(1)} %bitcast.94), kind=kLoop, calls=%fused_computation.1 | loop fusion | flops 5505024 | bytes 11010048 | tf_op jit(solution)/shard_map/stack | solution.py:637
  80.9 50.5 %shard_map.148 = (bf16[3,224,256]{2,1,0:T(8,128)(2,1)}, bf16[4,8,3584]{2,1,0:T(8,128)(2,1)}) custom-call(bf16[3,16,224,256]{3,2,1,0:T(8,128)(2,1)} %pad_maximum_fusion.g_in, bf16[16,2,8,3584]{3,2,1,0:T(8,128)(2,1)} %bitcast.96), custom_call_target="tpu_custom_call" | custom-call | tf_op jit(solution)/shard_map/pallas_call | solution.py:514
  131.4 2.3 %convolution_convert_fusion.3 = bf16[128,3584]{1,0:T(8,128)(2,1)} fusion(bf16[128,32]{0,1:T(8,128)(2,1)S(1)} %bitcast.110, bf16[4,8,3584]{2,1,0:T(8,128)(2,1)} %get-tuple-element.10), kind=kOutput, calls=%fused_computation.6 | convolution fusion | flops 29818880 | bytes 1155072 | tf_op jit(solution)/shard_map/dot_general | solution.py:648
  133.7 1.7 %slice_bitcast_fusion = (bf16[256,224]{0,1:T(8,128)(2,1)}, bf16[224,256]{1,0:T(8,128)(2,1)}, bf16[224,256]{1,0:T(8,128)(2,1)}) fusion(bf16[3,224,256]{2,1,0:T(8,128)(2,1)} %get-tuple-element.11), kind=kLoop, calls=%fused_computation.30 | loop fusion | bytes 688128 | tf_op jit(solution)/shard_map/transpose | solution.py:651
  (44 shorter events, 2.4 us)
Async XLA Ops:
  0.6 3.8 %copy-start = (bf16[128,3584]{1,0:T(8,128)(2,1)S(1)}, bf16[128,3584]{1,0:T(8,128)(2,1)}, u32[]{:S(2)}) copy-start(bf16[128,3584]{1,0:T(8,128)(2,1)} %param.13) | copy-start | bytes 2752516
  0.6 4.1 %copy-start.2 = (bf16[128,3584]{1,0:T(8,128)(2,1)S(1)}, bf16[128,3584]{1,0:T(8,128)(2,1)}, u32[]{:S(2)}) copy-start(bf16[128,3584]{1,0:T(8,128)(2,1)} %param.12) | copy-start | bytes 2752516
  3.2 2.7 %copy-start.6 = (f32[28,2]{0,1:T(2,128)S(1)}, f32[28,2]{0,1:T(2,128)}, u32[]{:S(2)}) copy-start(f32[28,2]{0,1:T(2,128)} %param.21) | copy-start | bytes 676
  3.2 2.8 %copy-start.7 = (f32[28,2]{0,1:T(2,128)S(1)}, f32[28,2]{0,1:T(2,128)}, u32[]{:S(2)}) copy-start(f32[28,2]{0,1:T(2,128)} %param.22) | copy-start | bytes 676
  3.3 2.9 %copy-start.8 = (f32[2,28]{1,0:T(2,128)S(1)}, f32[2,28]{1,0:T(2,128)}, u32[]{:S(2)}) copy-start(f32[2,28]{1,0:T(2,128)} %param.23) | copy-start | bytes 676
  4.8 2.5 %copy-start.3 = (bf16[224,256]{1,0:T(8,128)(2,1)S(1)}, bf16[224,256]{1,0:T(8,128)(2,1)}, u32[]{:S(2)}) copy-start(bf16[224,256]{1,0:T(8,128)(2,1)} %param.18) | copy-start | bytes 344068
  4.8 2.5 %copy-start.4 = (bf16[224,256]{1,0:T(8,128)(2,1)S(1)}, bf16[224,256]{1,0:T(8,128)(2,1)}, u32[]{:S(2)}) copy-start(bf16[224,256]{1,0:T(8,128)(2,1)} %param.19) | copy-start | bytes 344068
  5.1 2.7 %copy-start.5 = (bf16[256,224]{0,1:T(8,128)(2,1)S(1)}, bf16[256,224]{0,1:T(8,128)(2,1)}, u32[]{:S(2)}) copy-start(bf16[256,224]{0,1:T(8,128)(2,1)} %param.20) | copy-start | bytes 344068
  67.1 3.7 %copy-start.1 = (bf16[3,16,224,256]{3,2,1,0:T(8,128)(2,1)S(1)}, bf16[3,16,224,256]{3,2,1,0:T(8,128)(2,1)}, u32[]{:S(2)}) copy-start(bf16[3,16,224,256]{3,2,1,0:T(8,128)(2,1)} %get-tuple-element.9) | copy-start | bytes 16515076

commit v2 on v1

v2 whole, which is shorter than its diff:
```python
import functools

import jax
import jax.numpy as jnp
from jax import lax
from jax.experimental import pallas as pl
from jax.experimental.pallas import tpu as pltpu
from jax.sharding import PartitionSpec as P

HSH = 8
CAP = 4
BLOCK = 128
MESH = pl.DeviceIdType.MESH

NX = 4
NZ = 16
SEG = 4
ROWS = 2 * CAP

HALF = ((0, 112), (112, 112))
PART = (((0, 64), (64, 48)), ((112, 48), (160, 64)))

HOPS = 10


def passes_on(h, r, q):
    d = (h + 3 - q) // 4
    p = (q - h) % 4
    if r == 0:
        return d == 0 and q < 3
    if r == 1:
        return d == 0 or (d == 1 and q < 3)
    return p >= 2 and (d <= 1 or (d == 2 and q < 3))


def onward(h, r):
    return tuple(q for q in range(4) if passes_on(h, r, q))


def arrives(h, r):
    return tuple(q for q in range(4) if h > 0 and passes_on(h - 1, r, (q - 1) % 4))


def kept(h, r):
    return tuple(q for q in arrives(h, r) if (h + 3 - q) // 4 == r)


def lands(h, r):
    return tuple(q for q in onward(h, r) if (q + 1) % 4 in kept(h + 1, r))


def when_in(q, places, body):
    if not places:
        return
    if len(places) == 4:
        body()
        return
    test = q == places[0]
    for place in places[1:]:
        test = test | (q == place)
    pl.when(test)(body)


def place_of():
    g = lax.axis_index("dp")
    j = lax.axis_index("expert")
    return g // NX, g % NX, j // 2, j % 2


def greet(neighbours):
    barrier = pltpu.get_barrier_semaphore()
    for device in neighbours:
        pl.semaphore_signal(barrier, inc=1, device_id=device, device_id_type=MESH)
    pl.semaphore_wait(barrier, len(neighbours))


def at_offset(x, y, axis, offset):
    if axis == 0:
        return ((x + offset) % NX) * NX + y
    return x * NX + (y + offset) % NX


def block_at(x, y, half, i, k):
    if half == 0:
        return ((x + i) % NX) * NX + (y + k) % NX
    return ((x + k) % NX) * NX + (y + i) % NX


def remote(src, dst, send, recv, device):
    return pltpu.make_async_remote_copy(
        src_ref=src,
        dst_ref=dst,
        send_sem=send,
        recv_sem=recv,
        device_id=device,
        device_id_type=MESH,
    )


def gather_kernel(
    w_ref, rows_ref, full_ref, f_ref, u_ref, w_send, w_recv, z_send, z_recv, p_send, p_recv, own_sem
):
    x, y, z, c = place_of()
    g = x * NX + y
    j = z * 2 + c
    seg = z // SEG
    partner = (g, z * 2 + 1 - c)

    def across(axis, way):
        return (at_offset(x, y, axis, way), j)

    def along(way):
        return (g, ((z + way + NZ) % NZ) * 2 + c)

    greet(
        [across(0, 1), across(0, -1), across(1, 1), across(1, -1), along(1), along(-1), partner]
    )

    keep_w = pltpu.make_async_copy(w_ref, full_ref.at[:, g], own_sem.at[0])
    keep_rows = pltpu.make_async_copy(rows_ref.at[seg], f_ref.at[:, z, c], own_sem.at[1])

    def place(way):
        q = z % SEG
        return q if way == 1 else SEG - 1 - q

    def row_block(way, h, r):
        s = (z - way * h + NZ) % NZ
        e = (s // SEG + way * r + SEG) % SEG
        return s, e

    def row_copy(way, h, r, keeps, lands_kept):
        n = 0 if way == 1 else 1
        s, e = row_block(way, h, r)
        if h == 0:
            src = rows_ref.at[e]
        else:
            src = f_ref.at[:, s, c] if keeps else u_ref.at[e, :, s]
        dst = f_ref.at[:, s, c] if lands_kept else u_ref.at[e, :, s]
        return remote(src, dst, z_send.at[n, h, r], z_recv.at[n, h + 1, r], along(way))

    def row_arrival(way, h, r, keeps):
        n = 0 if way == 1 else 1
        s, e = row_block(way, h, r)
        slot = f_ref.at[:, s, c] if keeps else u_ref.at[e, :, s]
        return remote(slot, slot, z_send.at[n, h, r], z_recv.at[n, h, r], along(way))

    def share(way, h):
        n = 0 if way == 1 else 1
        s = (z - way * h + NZ) % NZ
        slot = f_ref.at[:, s, c]
        src = rows_ref.at[seg] if h == 0 else slot
        return remote(src, slot, p_send.at[n, h], p_recv.at[n, h], partner)

    def shared(way, h):
        n = 0 if way == 1 else 1
        s = (z - way * h + NZ) % NZ
        slot = f_ref.at[:, s, 1 - c]
        return remote(slot, slot, p_send.at[n, h], p_recv.at[n, h], partner)

    def row_step(h):
        for r in (2, 1, 0):
            for way in (1, -1):
                q = place(way)
                mine, on, to_kept = kept(h, r), onward(h, r), lands(h, r)
                through = tuple(p for p in arrives(h, r) if p not in mine)

                def arrived(keeps, way=way, r=r):
                    row_arrival(way, h, r, keeps).wait_recv()

                def go(keeps, lands_kept, way=way, r=r):
                    row_copy(way, h, r, keeps, lands_kept).start()

                when_in(q, mine, functools.partial(arrived, True))
                when_in(q, through, functools.partial(arrived, False))
                for keeps in (True, False):
                    for lands_kept in (True, False):
                        places = tuple(
                            p for p in on if (p in mine) == keeps and (p in to_kept) == lands_kept
                        )
                        when_in(q, places, functools.partial(go, keeps, lands_kept))
                when_in(q, mine, lambda way=way: share(way, h).start())

    def w_copy(half, stage, way, part):
        first, second = (0, 1) if half == 0 else (1, 0)
        axis = first if stage == 0 else second
        i = 0 if stage == 0 else (0, 1, -1, 2)[stage - 1]
        if part is None:
            start, size = HALF[half]
            back = 0
        else:
            start, size = PART[half][part]
            back = -way
        if stage == 0:
            owner = block_at(x, y, half, back, 0)
        else:
            owner = block_at(x, y, half, i, back)
        slot = full_ref.at[:, owner, pl.ds(start, size)]
        own = part is None and (stage == 0 or i == 0)
        src = w_ref.at[:, pl.ds(start, size)] if own else slot
        n = 2 * (0 if part is None else 1) + (0 if way == 1 else 1)
        return remote(
            src, slot, w_send.at[half, stage, n], w_recv.at[half, stage, n], across(axis, way)
        )

    def w_arrival(half, stage, way, part):
        first, second = (0, 1) if half == 0 else (1, 0)
        axis = first if stage == 0 else second
        i = 0 if stage == 0 else (0, 1, -1, 2)[stage - 1]
        start, size = HALF[half] if part is None else PART[half][part]
        back = -way if part is None else -2 * way
        owner = block_at(x, y, half, back, 0) if stage == 0 else block_at(x, y, half, i, back)
        slot = full_ref.at[:, owner, pl.ds(start, size)]
        n = 2 * (0 if part is None else 1) + (0 if way == 1 else 1)
        return remote(
            slot, slot, w_send.at[half, stage, n], w_recv.at[half, stage, n], across(axis, way)
        )

    def w_start(stage):
        for half in (0, 1):
            for way in (1, -1):
                w_copy(half, stage, way, None).start()

    def w_forward(stage, then=None):
        for way in (1, -1):
            for half in (0, 1):
                w_arrival(half, stage, way, None).wait_recv()
                w_copy(half, stage, way, 0 if way == 1 else 1).start()
                if then is not None:
                    for other in (1, -1):
                        w_copy(half, then[way], other, None).start()

    row_step(0)
    w_start(0)
    w_start(1)
    share(1, 0).start()
    keep_w.start()
    keep_rows.start()
    row_step(1)
    w_forward(0, {1: 3, -1: 2})
    row_step(2)
    w_forward(1)
    for half in (0, 1):
        for way in (1, -1):
            w_arrival(half, 0, way, 0 if way == 1 else 1).wait_recv()
    w_start(4)
    row_step(3)
    w_forward(3)
    row_step(4)
    w_forward(2)
    row_step(5)
    w_forward(4)
    for h in range(6, HOPS):
        row_step(h)

    for stage in range(5):
        for half in (0, 1):
            for way in (1, -1):
                part = 0 if way == 1 else 1
                if stage > 0:
                    w_arrival(half, stage, way, part).wait_recv()
                w_copy(half, stage, way, None).wait_send()
                w_copy(half, stage, way, part).wait_send()
    share(1, 0).wait_send()
    shared(1, 0).wait_recv()
    for h in range(HOPS):
        for way in (1, -1):
            q = place(way)
            for r in (2, 1, 0):
                when_in(
                    q,
                    onward(h, r),
                    lambda way=way, r=r: row_copy(way, h, r, False, False).wait_send(),
                )

                def end_share(way=way):
                    share(way, h).wait_send()
                    shared(way, h).wait_recv()

                when_in(q, kept(h, r), end_share)
    keep_w.wait()
    keep_rows.wait()


def gather(weights, rows):
    kinds, depth, hidden = weights.shape
    experts, streams, count, width = rows.shape
    dma = pltpu.SemaphoreType.DMA
    return pl.pallas_call(
        gather_kernel,
        out_shape=(
            jax.ShapeDtypeStruct((kinds, NX * NX, depth, hidden), jnp.bfloat16),
            jax.ShapeDtypeStruct((streams, NZ, 2, count, width), jnp.bfloat16),
            jax.ShapeDtypeStruct((experts, streams, NZ, count, width), jnp.bfloat16),
        ),
        in_specs=[pl.BlockSpec(memory_space=pl.ANY)] * 2,
        out_specs=(pl.BlockSpec(memory_space=pl.ANY),) * 3,
        scratch_shapes=[
            dma((2, 5, 4)),
            dma((2, 5, 4)),
            dma((2, HOPS + 1, 3)),
            dma((2, HOPS + 1, 3)),
            dma((2, HOPS)),
            dma((2, HOPS)),
            dma((2,)),
        ],
        compiler_params=pltpu.CompilerParams(collective_id=0, has_side_effects=True),
    )(weights, rows)


REACH = 6
STAGE_OFFSETS = (0, 1, -1, 2)


def reduce_kernel(
    full_in,
    rows_in,
    grad_ref,
    out_ref,
    w,
    xc,
    xct,
    g_ref,
    dx_ref,
    v_part,
    v_whole,
    theirs,
    total,
    held,
    near,
    last,
    v_send,
    v_recv,
    e_send,
    e_recv,
    h_send,
    h_recv,
    l_recv,
    p_sem,
    in_sem,
):
    x, y, z, c = place_of()
    g = x * NX + y
    j = z * 2 + c
    seg = z // SEG
    partner = (g, z * 2 + 1 - c)
    f32 = jnp.float32
    bf16 = jnp.bfloat16
    kinds, depth = grad_ref.shape[:2]
    width = xc.shape[2]

    loads = [
        pltpu.make_async_copy(src, dst, in_sem.at[n])
        for n, (src, dst) in enumerate(
            (
                (rows_in.at[0], xc.at[0]),
                (rows_in.at[1], xc.at[1]),
                (full_in.at[0], w.at[0]),
                (full_in.at[1], w.at[1]),
                (full_in.at[2], w.at[2]),
            )
        )
    ]
    for load in loads:
        load.start()

    def across(axis, way):
        return (at_offset(x, y, axis, way), j)

    def along(offset):
        return (g, ((z + offset + NZ) % NZ) * 2 + c)

    greet(
        [across(0, 1), across(0, -1), across(1, 1), across(1, -1), partner]
        + [along(way * t) for t in range(1, REACH + 1) for way in (1, -1)]
    )

    def owner_of(half, stage, back):
        if stage == 0:
            return block_at(x, y, half, back, 0)
        return block_at(x, y, half, STAGE_OFFSETS[stage - 1], back)

    def axis_of(half, stage):
        first, second = (0, 1) if half == 0 else (1, 0)
        return first if stage == 0 else second

    def g_part(m, half, stage, way):
        k = 0 if way == 1 else 1
        start, size = PART[half][k]
        return remote(
            g_ref.at[m, owner_of(half, stage, 2), pl.ds(start, size)],
            v_part.at[half, stage, k, m, pl.ds(0, size)],
            v_send.at[half, stage, k, m],
            v_recv.at[half, stage, k, m],
            across(axis_of(half, stage), way),
        )

    def g_whole(m, half, stage, way):
        k = 0 if way == 1 else 1
        start, size = HALF[half]
        return remote(
            g_ref.at[m, owner_of(half, stage, way), pl.ds(start, size)],
            v_whole.at[half, stage, k, m],
            v_send.at[half, stage, 2 + k, m],
            v_recv.at[half, stage, 2 + k, m],
            across(axis_of(half, stage), way),
        )

    def parts_in(stage):
        def one(m, _):
            for half in (0, 1):
                for way in (1, -1):
                    k = 0 if way == 1 else 1
                    start, size = PART[half][k]
                    g_part(m, half, stage, way).wait_recv()
                    block = owner_of(half, stage, way)
                    here = g_ref[m, block, pl.ds(start, size), :].astype(f32)
                    came = v_part[half, stage, k, m, pl.ds(0, size), :].astype(f32)
                    g_ref[m, block, pl.ds(start, size), :] = (here + came).astype(bf16)
                    g_whole(m, half, stage, way).start()
            return 0

        lax.fori_loop(0, kinds, one, 0)

    def wholes_in(stage, then=False):
        def one(m, _):
            for half in (0, 1):
                start, size = HALF[half]
                g_whole(m, half, stage, 1).wait_recv()
                g_whole(m, half, stage, -1).wait_recv()
                block = owner_of(half, stage, 0)
                here = g_ref[m, block, pl.ds(start, size), :].astype(f32)
                left = v_whole[half, stage, 0, m].astype(f32)
                right = v_whole[half, stage, 1, m].astype(f32)
                summed = (here + left + right).astype(bf16)
                if stage == 0:
                    grad_ref[m, pl.ds(start, size), :] = summed
                else:
                    g_ref[m, block, pl.ds(start, size), :] = summed
                if then:
                    for way in (1, -1):
                        g_part(m, half, 0, way).start()
            return 0

        lax.fori_loop(0, kinds, one, 0)

    def place(way):
        q = z % SEG
        return q if way == 1 else SEG - 1 - q

    def slots(way, kind, n):
        side = 0 if way == 1 else 1
        if kind == "near":
            return near.at[side, n], h_recv.at[side, n]
        if kind == "held":
            return held.at[side, n], e_recv.at[side, n]
        return last.at[side, n], l_recv.at[side, n]

    def item_sem(way, kind, n):
        side = 0 if way == 1 else 1
        return h_send.at[side, n] if kind == "near" else e_send.at[side, n]

    def await_item(way, kind, n):
        slot, recv = slots(way, kind, n)
        remote(slot, slot, recv, recv, along(way)).wait_recv()

    def send_item(way, kind, n, q):
        s = (z - way * (n if kind == "near" else q + n) + 2 * NZ) % NZ
        src = total.at[s] if q == SEG - 1 else slots(way, kind, n)[0]
        if kind == "near":
            dst, recv = slots(way, "near", n - 1) if n > 1 else slots(way, "last", 0)
            target = along(-way)
        elif q > 0:
            dst, recv = slots(way, "held", n)
            target = along(-way)
        else:
            dst, recv = slots(way, "last", 1 if n <= SEG else 2)
            target = along(-way * n)
        return remote(src, dst, item_sem(way, kind, n), recv, target)

    def items_of(q):
        return [("held", t) for t in range(REACH, 0, -1)] + [("near", h) for h in range(q, 0, -1)]

    def item_step(way, kind, n, q):
        if q < SEG - 1:
            side = 0 if way == 1 else 1
            s = (z - way * (n if kind == "near" else q + n) + 2 * NZ) % NZ
            await_item(way, kind, n)
            slot = near if kind == "near" else held
            slot[side, n] = (slot[side, n].astype(f32) + total[s].astype(f32)).astype(bf16)
        send_item(way, kind, n, q).start()

    def back_round(depth_from_far):
        for way in (1, -1):
            q = SEG - 1 - depth_from_far

            def go(way=way, q=q):
                for kind, n in items_of(q):
                    item_step(way, kind, n, q)

            pl.when(place(way) == q)(go)

    loads[0].wait()
    loads[1].wait()

    def turn(n, _):
        at = pl.ds(pl.multiple_of(n * 256, 256), 256)
        xct[0, at, :] = xc[0, :, at].T
        xct[1, at, :] = xc[1, :, at].T
        return 0

    lax.fori_loop(0, width // 256, turn, 0)
    loads[2].wait()
    gate_pre = jnp.dot(xc[0], w[0], preferred_element_type=f32)
    loads[3].wait()
    up_pre = jnp.dot(xc[0], w[1], preferred_element_type=f32)
    loads[4].wait()
    d_hidden = jnp.dot(xc[1], w[2], preferred_element_type=f32)
    gate_sig = jax.nn.sigmoid(gate_pre)
    swish = gate_pre * gate_sig
    hidden = (swish * up_pre).astype(bf16)
    d_up = (d_hidden * swish).astype(bf16)
    d_gate = (d_hidden * up_pre * gate_sig * (1.0 + gate_pre * (1.0 - gate_sig))).astype(bf16)

    def block_terms(i, k):
        block = block_at(x, y, 0, i, k)
        at = pl.ds(pl.multiple_of(block * depth, 16), depth)
        for m, (stream, right) in enumerate(((0, d_gate), (0, d_up), (1, hidden))):
            g_ref[m, block] = jnp.dot(xct[stream, at, :], right, preferred_element_type=f32).astype(
                bf16
            )
            if k == 2:
                stage = 1 + STAGE_OFFSETS.index(i)
                g_part(m, 0, stage, 1).start()
                g_part(m, 0, stage, -1).start()
            if i == 2:
                stage = 1 + STAGE_OFFSETS.index(k)
                g_part(m, 1, stage, 1).start()
                g_part(m, 1, stage, -1).start()

    first_blocks = ((2, 2), (1, 2), (2, 1), (-1, 2), (2, -1), (0, 2), (2, 0))
    for i, k in first_blocks:
        block_terms(i, k)

    by_hidden = (((1,), (1,)), ((), ()))
    chunk = 512

    def dx_chunk(n, _):
        at = pl.ds(pl.multiple_of(n * chunk, chunk), chunk)
        part = lax.dot_general(d_gate, w[0, at, :], by_hidden, preferred_element_type=f32)
        part = part + lax.dot_general(d_up, w[1, at, :], by_hidden, preferred_element_type=f32)
        dx_ref[:, :, :, at] = part.reshape(NZ, 2, ROWS, chunk).astype(bf16)
        return 0

    lax.fori_loop(0, width // chunk, dx_chunk, 0)
    swap = remote(dx_ref.at[:, 1 - c], theirs, p_sem.at[0], p_sem.at[1], partner)
    swap.start()
    for i in (1, -1, 0):
        for k in (1, -1, 0):
            block_terms(i, k)

    parts_in(4)
    swap.wait()

    def own_total(s, _):
        total[s] = (dx_ref[s, c].astype(f32) + theirs[s].astype(f32)).astype(bf16)
        return 0

    lax.fori_loop(0, NZ, own_total, 0)
    back_round(0)
    parts_in(2)
    back_round(1)
    parts_in(3)
    wholes_in(4, True)
    back_round(2)
    parts_in(1)
    back_round(3)
    wholes_in(2)
    wholes_in(3)
    parts_in(0)

    out_ref[seg] = total[z]

    def take(way, n):
        side = 0 if way == 1 else 1
        await_item(way, "last", n)
        if n == 0:
            out_ref[seg] = (out_ref[seg].astype(f32) + last[side, 0].astype(f32)).astype(bf16)
        else:
            out_ref[(seg + way * n + SEG) % SEG] = last[side, n]

    for way in (1, -1):
        when_in(place(way), (0, 1, 2), functools.partial(take, way, 0))
        take(way, 1)
        when_in(place(way), (2, 3), functools.partial(take, way, 2))

    wholes_in(1)
    wholes_in(0)

    def sent(m, _):
        for stage in range(5):
            for half in (0, 1):
                for way in (1, -1):
                    g_part(m, half, stage, way).wait_send()
                    g_whole(m, half, stage, way).wait_send()
        return 0

    lax.fori_loop(0, kinds, sent, 0)
    for way in (1, -1):
        for q in range(SEG):

            def ended(way=way, q=q):
                for kind, n in items_of(q):
                    send_item(way, kind, n, q).wait_send()

            pl.when(place(way) == q)(ended)


def layer_and_reduce(full, rows):
    kinds, whole_depth, hidden = full.shape
    streams, count, width = rows.shape
    groups = NX * NX
    depth = whole_depth // groups
    dma = pltpu.SemaphoreType.DMA
    vmem = pltpu.VMEM
    bf16 = jnp.bfloat16
    return pl.pallas_call(
        reduce_kernel,
        out_shape=(
            jax.ShapeDtypeStruct((kinds, depth, hidden), bf16),
            jax.ShapeDtypeStruct((SEG, ROWS, width), bf16),
        ),
        in_specs=[pl.BlockSpec(memory_space=pl.ANY)] * 2,
        out_specs=(pl.BlockSpec(memory_space=pltpu.VMEM),) * 2,
        scratch_shapes=[
            vmem((kinds, whole_depth, hidden), bf16),
            vmem((streams, count, width), bf16),
            vmem((streams, width, count), bf16),
            vmem((kinds, groups, depth, hidden), bf16),
            vmem((NZ, 2, ROWS, width), bf16),
            vmem((2, 5, 2, kinds, 64, hidden), bf16),
            vmem((2, 5, 2, kinds, 112, hidden), bf16),
            vmem((NZ, ROWS, width), bf16),
            vmem((NZ, ROWS, width), bf16),
            vmem((2, REACH + 1, ROWS, width), bf16),
            vmem((2, SEG, ROWS, width), bf16),
            vmem((2, 3, ROWS, width), bf16),
            dma((2, 5, 4, 3)),
            dma((2, 5, 4, 3)),
            dma((2, REACH + 1)),
            dma((2, REACH + 1)),
            dma((2, SEG)),
            dma((2, SEG)),
            dma((2, 3)),
            dma((2,)),
            dma((5,)),
        ],
        compiler_params=pltpu.CompilerParams(collective_id=1, has_side_effects=True),
    )(full, rows)


def route_rows(tokens, cotangent, route_weight, expert_ids, live_count, plan, experts, capacity):
    count = tokens.shape[0]
    token_index = jnp.arange(count, dtype=jnp.int32)
    expert_index = jnp.arange(experts, dtype=jnp.int32)
    matches = expert_ids[:, None, :] == expert_index[None, :, None]
    routed = jnp.any(matches, axis=2) & (token_index < live_count)[:, None]
    to_replica = (token_index % 2 == 1)[:, None] & (plan[None, :] == 1)
    in_lists = jnp.stack([routed & ~to_replica, routed & to_replica], axis=2).astype(jnp.int32)
    position = jnp.cumsum(in_lists, axis=0) - 1
    capacity_index = jnp.arange(capacity, dtype=jnp.int32)
    selected = ((in_lists[..., None] == 1) & (position[..., None] == capacity_index)).astype(
        jnp.float32
    )
    weight_sum = jnp.sum(jnp.where(matches, route_weight[:, None, :], jnp.float32(0.0)), axis=2)
    row_weight = jnp.sum(selected * weight_sum[:, :, None, None], axis=0)
    flat = selected.reshape(count, -1)
    picker = flat.T.astype(jnp.bfloat16)
    token_rows = jnp.dot(picker, tokens, preferred_element_type=jnp.float32).astype(jnp.bfloat16)
    cot_picked = jnp.dot(picker, cotangent, preferred_element_type=jnp.float32)
    cot_rows = (row_weight.reshape(-1, 1) * cot_picked).astype(jnp.bfloat16)
    shape = (experts, 2 * capacity, tokens.shape[1])
    return flat, jnp.stack([token_rows.reshape(shape), cot_rows.reshape(shape)], axis=1)


def scaled(values, scale, first_row):
    rows, hidden = values.shape
    blocks = (first_row + jnp.arange(rows, dtype=jnp.int32)) // BLOCK
    pick = (blocks[:, None] == jnp.arange(scale.shape[0], dtype=jnp.int32)[None, :])[:, :, None]
    of_row = jnp.sum(jnp.where(pick, scale[None], jnp.float32(0.0)), axis=1)
    spread = jnp.repeat(of_row, hidden // scale.shape[1], axis=1)
    return (values.astype(jnp.float32) * spread).astype(jnp.bfloat16)


def on_device(
    tokens,
    cotangent,
    route_weight,
    expert_ids,
    live_tokens,
    replica_plan,
    w_gate,
    w_up,
    w_down,
    scale_gate,
    scale_up,
    scale_down,
):
    members = lax.axis_size("expert")
    slot_count = members // HSH
    width = tokens.shape[1]
    first_row = lax.axis_index("dp") * w_gate.shape[0]
    weights = jnp.stack(
        [
            scaled(w_gate, scale_gate, first_row),
            scaled(w_up, scale_up, first_row),
            scaled(w_down.T, scale_down.T, first_row),
        ]
    )
    flat, rows = route_rows(
        tokens,
        cotangent,
        route_weight,
        expert_ids,
        live_tokens[0],
        replica_plan[0],
        slot_count,
        CAP,
    )
    full, arrived, _ = gather(weights, rows)
    grads, dx_rows = layer_and_reduce(
        full.reshape(full.shape[0], -1, full.shape[-1]), arrived.reshape(2, -1, width)
    )
    bf16, f32 = jnp.bfloat16, jnp.float32
    d_tokens = jnp.dot(
        flat.astype(bf16), dx_rows.reshape(-1, width), preferred_element_type=f32
    ).astype(bf16)
    return (d_tokens, grads[0], grads[1], grads[2].T)


def solution(mesh):
    return jax.shard_map(
        on_device,
        mesh=mesh,
        in_specs=(
            P(("dp", "expert"), None),
            P(("dp", "expert"), None),
            P(("dp", "expert"), None),
            P(("dp", "expert"), None),
            P(("dp", "expert")),
            P(("dp", "expert"), None),
            P("dp", "expert"),
            P("dp", "expert"),
            P("expert", "dp"),
            P(None, "expert"),
            P(None, "expert"),
            P("expert", None),
        ),
        out_specs=(
            P(("dp", "expert"), None),
            P("dp", "expert"),
            P("dp", "expert"),
            P("expert", "dp"),
        ),
        check_vma=False,
    )
```

time: 136 us -> 132 us (0.971)
  the two profiles are of different devices: /device:TPU:38 before, /device:TPU:8 now
where the time goes in v2:
time: 132 us
  Pallas kernels  116 us (88%)
  local copies, waits for them, and re-layouts  5.81 us (4%)
  other arithmetic  4.35 us (3%)
  matrix products  4.07 us (3%)
  between operations  1.56 us (1%)
    pallas_call x1, Pallas kernels, gather(): pl.pallas_call(gather_kernel, out_shape=(jax.ShapeDtypeStruct((kinds, NX...  63.3 us
    pallas_call x1, Pallas kernels, layer_and_reduce(): pl.pallas_call(reduce_kernel, out_shape=(jax.ShapeDtypeStruct((kinds, dep...  52.6 us

profile of v2, /device:TPU:8, one launch (start us, length us, event | category | flops | bytes accessed | tf_op | source)
XLA Modules:
  0.0 131.6 jit_solution(4956673284045044785)
XLA Ops:
  1.4 0.7 compare_bitcast_fusion
  2.1 0.7 fusion.10
  2.9 0.2 copy.30
  3.1 0.1 broadcast_add_fusion
  3.3 0.7 select_reduce_fusion.4
  4.1 0.1 select_reduce_fusion.3
  4.4 0.3 fusion.2
  4.7 1.5 %fusion.1 = bf16[4,1,8,3584]{3,2,1,0:T(8,128)(2,1)S(1)} fusion(bf16[128,3584]{1,0:T(8,128)(2,1)} %param.12, pred[128,32]{0,1:T(8,128)(4,1)S(1)} %bitcast.74, s32[128,32]{0,1:T(8,128)S(1)} %bitcast.72, s32[32]{0:T(128)S(1)} %eq.114), kind=kOutput, calls=%fused_computation.4 | convolution fusion | flops 29491200 | bytes 1167488 | tf_op jit(solution)/shard_map/dot_general | solution.py:678
  6.2 0.8 pad_maximum_fusion.rows_ref
  7.0 0.8 copy.32
  7.8 0.8 copy.34
  8.5 0.8 copy.36
  9.3 0.2 select_reduce_fusion.2
  9.5 0.1 copy.33
  9.6 0.3 broadcast_in_dim.83
  9.9 0.1 copy.35
  10.1 0.3 broadcast_in_dim.85
  10.5 0.1 copy.37
  10.6 0.3 broadcast_in_dim.87
  11.0 0.8 pad_maximum_fusion.1.w_ref
  11.7 63.3 %shard_map.147 = (bf16[3,16,224,256]{3,2,1,0:T(8,128)(2,1)}, bf16[2,16,2,8,3584]{4,3,2,1,0:T(8,128)(2,1)}, bf16[4,2,16,8,3584]{4,3,2,1,0:T(8,128)(2,1)}) custom-call(bf16[3,224,256]{2,1,0:T(8,128)(2,1)} %pad_maximum_fusion.1.w_ref, bf16[4,2,8,3584]{3,2,1,0:T(8,128)(2,1)} %pad_maximum_fusion.rows_ref), custom_call_target="tpu_custom_call" | custom-call | tf_op jit(solution)/shard_map/pallas_call | solution.py:288
  75.0 52.6 %shard_map.148 = (bf16[3,224,256]{2,1,0:T(8,128)(2,1)}, bf16[4,8,3584]{2,1,0:T(8,128)(2,1)}) custom-call(bf16[3,3584,256]{2,1,0:T(8,128)(2,1)} %bitcast.66, bf16[2,256,3584]{2,1,0:T(8,128)(2,1)} %bitcast.67), custom_call_target="tpu_custom_call" | custom-call | tf_op jit(solution)/shard_map/pallas_call | solution.py:626
  127.6 2.3 %convolution_convert_fusion = bf16[128,3584]{1,0:T(8,128)(2,1)} fusion(bf16[128,32]{0,1:T(8,128)(2,1)S(1)} %bitcast.75, bf16[4,8,3584]{2,1,0:T(8,128)(2,1)} %get-tuple-element.10), kind=kOutput, calls=%fused_computation | convolution fusion | flops 29818880 | bytes 1155072 | tf_op jit(solution)/shard_map/dot_general | solution.py:734
  129.9 1.7 %slice_bitcast_fusion = (bf16[256,224]{0,1:T(8,128)(2,1)}, bf16[224,256]{1,0:T(8,128)(2,1)}, bf16[224,256]{1,0:T(8,128)(2,1)}) fusion(bf16[3,224,256]{2,1,0:T(8,128)(2,1)} %get-tuple-element.11), kind=kLoop, calls=%fused_computation.19 | loop fusion | bytes 688128 | tf_op jit(solution)/shard_map/transpose | solution.py:737
  (23 shorter events, 0.5 us)
Async XLA Ops:
  0.6 3.7 %copy-start = (bf16[128,3584]{1,0:T(8,128)(2,1)S(1)}, bf16[128,3584]{1,0:T(8,128)(2,1)}, u32[]{:S(2)}) copy-start(bf16[128,3584]{1,0:T(8,128)(2,1)} %param.13) | copy-start | bytes 2752516
  0.6 9.7 %copy-start.1 = (bf16[224,256]{1,0:T(8,128)(2,1)S(1)}, bf16[224,256]{1,0:T(8,128)(2,1)}, u32[]{:S(2)}) copy-start(bf16[224,256]{1,0:T(8,128)(2,1)} %param.18) | copy-start | bytes 344068
  0.7 9.7 %copy-start.2 = (bf16[224,256]{1,0:T(8,128)(2,1)S(1)}, bf16[224,256]{1,0:T(8,128)(2,1)}, u32[]{:S(2)}) copy-start(bf16[224,256]{1,0:T(8,128)(2,1)} %param.19) | copy-start | bytes 344068
  0.7 10.2 %copy-start.3 = (bf16[256,224]{0,1:T(8,128)(2,1)S(1)}, bf16[256,224]{0,1:T(8,128)(2,1)}, u32[]{:S(2)}) copy-start(bf16[256,224]{0,1:T(8,128)(2,1)} %param.20) | copy-start | bytes 344068

commit v3 on v2

--- a/solution.py
+++ b/solution.py
@@ -314,8 +314,13 @@
 def reduce_kernel(
     full_in,
     rows_in,
+    pick_ref,
+    d_tokens_ref,
+    grad_gate_ref,
+    grad_up_ref,
+    grad_down_ref,
+    out_ref,
     grad_ref,
-    out_ref,
     w,
     xc,
     xct,
@@ -538,9 +543,6 @@
                 g_part(m, 1, stage, -1).start()
 
     first_blocks = ((2, 2), (1, 2), (2, 1), (-1, 2), (2, -1), (0, 2), (2, 0))
-    for i, k in first_blocks:
-        block_terms(i, k)
-
     by_hidden = (((1,), (1,)), ((), ()))
     chunk = 512
 
@@ -554,27 +556,29 @@
     lax.fori_loop(0, width // chunk, dx_chunk, 0)
     swap = remote(dx_ref.at[:, 1 - c], theirs, p_sem.at[0], p_sem.at[1], partner)
     swap.start()
+    for i, k in first_blocks:
+        block_terms(i, k)
+    swap.wait()
+
+    def own_total(s, _):
+        total[s] = (dx_ref[s, c].astype(f32) + theirs[s].astype(f32)).astype(bf16)
+        return 0
+
+    lax.fori_loop(0, NZ, own_total, 0)
+    back_round(0)
     for i in (1, -1, 0):
         for k in (1, -1, 0):
             block_terms(i, k)
 
     parts_in(4)
-    swap.wait()
-
-    def own_total(s, _):
-        total[s] = (dx_ref[s, c].astype(f32) + theirs[s].astype(f32)).astype(bf16)
-        return 0
-
-    lax.fori_loop(0, NZ, own_total, 0)
-    back_round(0)
     parts_in(2)
+    parts_in(3)
     back_round(1)
-    parts_in(3)
     wholes_in(4, True)
+    parts_in(1)
     back_round(2)
-    parts_in(1)
+    wholes_in(2)
     back_round(3)
-    wholes_in(2)
     wholes_in(3)
     parts_in(0)
 
@@ -594,7 +598,16 @@
         when_in(place(way), (2, 3), functools.partial(take, way, 2))
 
     wholes_in(1)
+    d_tokens_ref[...] = lax.dot_general(
+        pick_ref[...],
+        out_ref[...].astype(f32).reshape(SEG * ROWS, width).astype(bf16),
+        (((0,), (0,)), ((), ())),
+        preferred_element_type=f32,
+    ).astype(bf16)
     wholes_in(0)
+    grad_gate_ref[...] = grad_ref[0]
+    grad_up_ref[...] = grad_ref[1]
+    grad_down_ref[...] = grad_ref[2]
 
     def sent(m, _):
         for stage in range(5):
@@ -615,7 +628,7 @@
             pl.when(place(way) == q)(ended)
 
 
-def layer_and_reduce(full, rows):
+def layer_and_reduce(full, rows, picker):
     kinds, whole_depth, hidden = full.shape
     streams, count, width = rows.shape
     groups = NX * NX
@@ -626,12 +639,17 @@
     return pl.pallas_call(
         reduce_kernel,
         out_shape=(
-            jax.ShapeDtypeStruct((kinds, depth, hidden), bf16),
-            jax.ShapeDtypeStruct((SEG, ROWS, width), bf16),
+            jax.ShapeDtypeStruct((picker.shape[1], width), bf16),
+            jax.ShapeDtypeStruct((depth, hidden), bf16),
+            jax.ShapeDtypeStruct((depth, hidden), bf16),
+            jax.ShapeDtypeStruct((depth, hidden), bf16),
         ),
-        in_specs=[pl.BlockSpec(memory_space=pl.ANY)] * 2,
-        out_specs=(pl.BlockSpec(memory_space=pltpu.VMEM),) * 2,
+        in_specs=[pl.BlockSpec(memory_space=pl.ANY)] * 2
+        + [pl.BlockSpec(memory_space=pltpu.VMEM)],
+        out_specs=(pl.BlockSpec(memory_space=pltpu.VMEM),) * 4,
         scratch_shapes=[
+            vmem((SEG, ROWS, width), bf16),
+            vmem((kinds, depth, hidden), bf16),
             vmem((kinds, whole_depth, hidden), bf16),
             vmem((streams, count, width), bf16),
             vmem((streams, width, count), bf16),
@@ -655,40 +673,102 @@
             dma((5,)),
         ],
         compiler_params=pltpu.CompilerParams(collective_id=1, has_side_effects=True),
-    )(full, rows)
-
-
-def route_rows(tokens, cotangent, route_weight, expert_ids, live_count, plan, experts, capacity):
-    count = tokens.shape[0]
-    token_index = jnp.arange(count, dtype=jnp.int32)
-    expert_index = jnp.arange(experts, dtype=jnp.int32)
-    matches = expert_ids[:, None, :] == expert_index[None, :, None]
-    routed = jnp.any(matches, axis=2) & (token_index < live_count)[:, None]
-    to_replica = (token_index % 2 == 1)[:, None] & (plan[None, :] == 1)
-    in_lists = jnp.stack([routed & ~to_replica, routed & to_replica], axis=2).astype(jnp.int32)
-    position = jnp.cumsum(in_lists, axis=0) - 1
-    capacity_index = jnp.arange(capacity, dtype=jnp.int32)
-    selected = ((in_lists[..., None] == 1) & (position[..., None] == capacity_index)).astype(
-        jnp.float32
-    )
-    weight_sum = jnp.sum(jnp.where(matches, route_weight[:, None, :], jnp.float32(0.0)), axis=2)
-    row_weight = jnp.sum(selected * weight_sum[:, :, None, None], axis=0)
-    flat = selected.reshape(count, -1)
-    picker = flat.T.astype(jnp.bfloat16)
-    token_rows = jnp.dot(picker, tokens, preferred_element_type=jnp.float32).astype(jnp.bfloat16)
-    cot_picked = jnp.dot(picker, cotangent, preferred_element_type=jnp.float32)
-    cot_rows = (row_weight.reshape(-1, 1) * cot_picked).astype(jnp.bfloat16)
-    shape = (experts, 2 * capacity, tokens.shape[1])
-    return flat, jnp.stack([token_rows.reshape(shape), cot_rows.reshape(shape)], axis=1)
-
-
-def scaled(values, scale, first_row):
-    rows, hidden = values.shape
-    blocks = (first_row + jnp.arange(rows, dtype=jnp.int32)) // BLOCK
-    pick = (blocks[:, None] == jnp.arange(scale.shape[0], dtype=jnp.int32)[None, :])[:, :, None]
-    of_row = jnp.sum(jnp.where(pick, scale[None], jnp.float32(0.0)), axis=1)
-    spread = jnp.repeat(of_row, hidden // scale.shape[1], axis=1)
-    return (values.astype(jnp.float32) * spread).astype(jnp.bfloat16)
+    )(full, rows, picker)
+
+
+def prepare_kernel(
+    live_ref,
+    plan_ref,
+    scale_gate_ref,
+    scale_up_ref,
+    scale_down_ref,
+    ids_ref,
+    weight_ref,
+    tokens_ref,
+    cot_ref,
+    gate_ref,
+    up_ref,
+    down_ref,
+    w_ref,
+    rows_ref,
+    pick_ref,
+):
+    f32 = jnp.float32
+    bf16 = jnp.bfloat16
+    experts = plan_ref.shape[1]
+    count = tokens_ref.shape[0]
+    listed = experts * ROWS
+    zero = jnp.float32(0.0)
+
+    slot = lax.broadcasted_iota(jnp.int32, (1, count), 1)
+    live = slot < live_ref[0]
+    odd = slot % 2 == 1
+    row = lax.broadcasted_iota(jnp.int32, (listed, count), 0)
+    member = jnp.zeros((listed, count), f32)
+    weight = jnp.zeros((listed, count), f32)
+    ids = ids_ref[...]
+    for e in range(experts):
+        match = ids == e
+        routed = jnp.sum(jnp.where(match, 1.0, 0.0), axis=0, keepdims=True)
+        routed = jnp.where(live & (routed > 0.0), 1.0, 0.0)
+        weight_sum = jnp.sum(jnp.where(match, weight_ref[...], zero), axis=0, keepdims=True)
+        weight = jnp.where(row // ROWS == e, weight_sum, weight)
+        split = jnp.where(plan_ref[0, e] == 1, 1.0, 0.0)
+        second = routed * jnp.where(odd, split, 0.0)
+        member = jnp.where(row // CAP == 2 * e, routed - second, member)
+        member = jnp.where(row // CAP == 2 * e + 1, second, member)
+    before = lax.broadcasted_iota(jnp.int32, (count, count), 0)
+    after = lax.broadcasted_iota(jnp.int32, (count, count), 1)
+    ladder = jnp.where(before <= after, 1.0, 0.0).astype(bf16)
+    nth = jnp.dot(member.astype(bf16), ladder, preferred_element_type=f32)
+    chosen = (member > 0.5) & (nth == (row % CAP + 1).astype(f32))
+    chosen = jnp.where(chosen, 1.0, 0.0)
+    picker = chosen.astype(bf16)
+    pick_ref[...] = picker
+    row_weight = jnp.sum(chosen * weight, axis=1, keepdims=True)
+    token_rows = jnp.dot(picker, tokens_ref[...], preferred_element_type=f32)
+    cot_rows = row_weight * jnp.dot(picker, cot_ref[...], preferred_element_type=f32)
+    for e in range(experts):
+        rows_ref[e, 0] = token_rows[e * ROWS : (e + 1) * ROWS].astype(bf16)
+        rows_ref[e, 1] = cot_rows[e * ROWS : (e + 1) * ROWS].astype(bf16)
+
+    depth = gate_ref.shape[0]
+    first = lax.axis_index("dp") * depth
+    base = first // BLOCK
+    block = (first + lax.broadcasted_iota(jnp.int32, (depth, BLOCK), 0)) // BLOCK - base
+    for m, (values, scale) in enumerate(
+        ((gate_ref, scale_gate_ref), (up_ref, scale_up_ref), (down_ref, scale_down_ref))
+    ):
+        most = scale.shape[1] - 1
+        for part in range(scale.shape[0]):
+            at = pl.ds(part * BLOCK, BLOCK)
+            spread = jnp.where(
+                block == 0,
+                scale[part, base],
+                jnp.where(
+                    block == 1,
+                    scale[part, jnp.minimum(base + 1, most)],
+                    scale[part, jnp.minimum(base + 2, most)],
+                ),
+            )
+            w_ref[m, :, at] = (values[:, at].astype(f32) * spread).astype(bf16)
+
+
+def prepare(tokens, cotangent, route_weight, expert_ids, live, plan, weights, scales):
+    count, width = tokens.shape
+    experts = plan.shape[1]
+    smem = pl.BlockSpec(memory_space=pltpu.SMEM)
+    vmem = pl.BlockSpec(memory_space=pltpu.VMEM)
+    return pl.pallas_call(
+        prepare_kernel,
+        out_shape=(
+            jax.ShapeDtypeStruct((len(weights),) + weights[0].shape, jnp.bfloat16),
+            jax.ShapeDtypeStruct((experts, 2, ROWS, width), jnp.bfloat16),
+            jax.ShapeDtypeStruct((experts * ROWS, count), jnp.bfloat16),
+        ),
+        in_specs=[smem] * 5 + [vmem] * 7,
+        out_specs=(vmem,) * 3,
+    )(live, plan, *scales, expert_ids.T, route_weight.T, tokens, cotangent, *weights)
 
 
 def on_device(
@@ -705,36 +785,22 @@
     scale_up,
     scale_down,
 ):
-    members = lax.axis_size("expert")
-    slot_count = members // HSH
     width = tokens.shape[1]
-    first_row = lax.axis_index("dp") * w_gate.shape[0]
-    weights = jnp.stack(
-        [
-            scaled(w_gate, scale_gate, first_row),
-            scaled(w_up, scale_up, first_row),
-            scaled(w_down.T, scale_down.T, first_row),
-        ]
-    )
-    flat, rows = route_rows(
+    weights, rows, picker = prepare(
         tokens,
         cotangent,
         route_weight,
         expert_ids,
-        live_tokens[0],
-        replica_plan[0],
-        slot_count,
-        CAP,
+        live_tokens,
+        replica_plan,
+        (w_gate, w_up, w_down.T),
+        (scale_gate.T, scale_up.T, scale_down),
     )
     full, arrived, _ = gather(weights, rows)
-    grads, dx_rows = layer_and_reduce(
-        full.reshape(full.shape[0], -1, full.shape[-1]), arrived.reshape(2, -1, width)
+    d_tokens, grad_gate, grad_up, grad_down = layer_and_reduce(
+        full.reshape(full.shape[0], -1, full.shape[-1]), arrived.reshape(2, -1, width), picker
     )
-    bf16, f32 = jnp.bfloat16, jnp.float32
-    d_tokens = jnp.dot(
-        flat.astype(bf16), dx_rows.reshape(-1, width), preferred_element_type=f32
-    ).astype(bf16)
-    return (d_tokens, grads[0], grads[1], grads[2].T)
+    return (d_tokens, grad_gate, grad_up, grad_down.T)
 
 
 def solution(mesh):

time: 132 us -> 124 us (0.939)
  other arithmetic: 4.35 us -> 0 us
  matrix products: 4.07 us -> 0 us
    unnamed x10 -> x4, local copies, waits for them, and re-layouts: 1.56 us -> 6.81 us
    dot_general x3 -> x0, matrix products: 4.07 us -> none  [the longest x1 2.28 us: on_device(): jnp.dot(flat.astype(bf16), dx_rows.reshape(-1, width), preferred_element_...]
    transpose x2 -> x0, local copies, waits for them, and re-layouts: 2.51 us -> none  [the longest x1 1.74 us: on_device(): return (d_tokens, grads[0], grads[1], grads[2].T)]
    another operation x5 -> x0, other arithmetic: 1.84 us -> none  [the longest x3 0.89 us: on_device(): jnp.stack([scaled(w_gate, scale_gate, first_row), scaled(w_up, scale_up,...]
    pallas_call x1 -> x2, Pallas kernels: 52.6 us -> 52 us  [the longest x1 48.9 us: layer_and_reduce(): pl.pallas_call(reduce_kernel, out_shape=(jax.ShapeDtypeStruct((picker.sha...]
where the time goes in v3:
time: 124 us; the launch traced here: 123 us
  Pallas kernels  115 us (93%)
  local copies, waits for them, and re-layouts  6.81 us (5%)
  between operations  1.3 us (1%)
    pallas_call x1, Pallas kernels, gather(): pl.pallas_call(gather_kernel, out_shape=(jax.ShapeDtypeStruct((kinds, NX...  63.3 us
    pallas_call x1, Pallas kernels, layer_and_reduce(): pl.pallas_call(reduce_kernel, out_shape=(jax.ShapeDtypeStruct((picker.sha...  48.9 us
    unnamed x4, local copies, waits for them, and re-layouts  6.81 us
    pallas_call x1, Pallas kernels, prepare(): pl.pallas_call(prepare_kernel, out_shape=(jax.ShapeDtypeStruct((len(weigh...  3.1 us

profile of v3, /device:TPU:8, one launch (start us, length us, event | category | flops | bytes accessed | tf_op | source)
XLA Modules:
  0.0 123.4 jit_solution(11749556702513097800)
XLA Ops:
  1.3 3.1 %shard_map.147 = (bf16[3,224,256]{2,1,0:T(8,128)(2,1)}, bf16[4,2,8,3584]{3,2,1,0:T(8,128)(2,1)}, bf16[32,128]{1,0:T(8,128)(2,1)}) custom-call(s32[1]{0:T(128)S(6)} %copy.20.live_ref, s32[1,4]{1,0:T(1,128)} %plan_ref.1, f32[2,28]{1,0:T(2,128)} %bitcast.14, f32[2,28]{1,0:T(2,128)} %bitcast.15, f32[2,28]{1,0:T(2,128)} %scale_down_ref.1, s32[8,128]{1,0:T(8,128)} %bitcast.12, ...), custom_call_target="tpu_custom_call" | custom-call | tf_op jit(solution)/shard_map/pallas_call | solution.py:762
  4.4 63.3 %shard_map.148 = (bf16[3,16,224,256]{3,2,1,0:T(8,128)(2,1)}, bf16[2,16,2,8,3584]{4,3,2,1,0:T(8,128)(2,1)}, bf16[4,2,16,8,3584]{4,3,2,1,0:T(8,128)(2,1)}) custom-call(bf16[3,224,256]{2,1,0:T(8,128)(2,1)} %get-tuple-element.13.w_ref, bf16[4,2,8,3584]{3,2,1,0:T(8,128)(2,1)} %get-tuple-element.14.rows_ref), custom_call_target="tpu_custom_call" | custom-call | tf_op jit(solution)/shard_map/pallas_call | solution.py:288
  67.7 48.9 %shard_map.149 = (bf16[128,3584]{1,0:T(8,128)(2,1)}, bf16[224,256]{1,0:T(8,128)(2,1)}, bf16[224,256]{1,0:T(8,128)(2,1)}, bf16[224,256]{1,0:T(8,128)(2,1)}) custom-call(bf16[3,3584,256]{2,1,0:T(8,128)(2,1)} %bitcast.8, bf16[2,256,3584]{2,1,0:T(8,128)(2,1)} %bitcast.9, bf16[32,128]{1,0:T(8,128)(2,1)} %get-tuple-element.17.pick_ref), custom_call_target="tpu_custom_call" | custom-call | tf_op jit(solution)/shard_map/pallas_call | solution.py:639
  116.6 2.2 %copy.21 = bf16[128,3584]{1,0:T(8,128)(2,1)} copy(bf16[128,3584]{1,0:T(8,128)(2,1)} %get-tuple-element.26) | data formatting | bytes 1835008
  118.8 1.6 %copy.22 = bf16[224,256]{1,0:T(8,128)(2,1)} copy(bf16[224,256]{1,0:T(8,128)(2,1)} %get-tuple-element.27) | data formatting | bytes 229376
  120.3 1.6 %copy.23 = bf16[224,256]{1,0:T(8,128)(2,1)} copy(bf16[224,256]{1,0:T(8,128)(2,1)} %get-tuple-element.28) | data formatting | bytes 229376
  121.9 1.6 %copy.24 = bf16[256,224]{0,1:T(8,128)(2,1)} copy(bf16[256,224]{0,1:T(8,128)(2,1)} %bitcast.10) | data formatting | bytes 229376
